TPU v7x, 128 devices: a whole 4x4x4 slice. The times are simulated.
128 devices in a mesh: section: 2 (over z_hi), hid: 16 (over x, z_lo, core), wid: 4 (over y).
Axes of the slice: x: 4, y: 4, z: 4 (z_hi: 2, z_lo: 2; z = z_hi * 2 + z_lo), core: 2. Of those that a mesh axis runs over, the one named last changes fastest.
Arguments:
- grad_out: float32 [2, 256, 6144], P(None, None, 'wid'), may hold values from -6 to 6
- weight_in: bfloat16 [2, 6144, 24576], P('section', 'wid', 'hid'), may hold values from -0.078125 to 0.078125
- weight_out: bfloat16 [2, 24576, 6144], P('section', 'hid', 'wid'), may hold values from -0.0390625 to 0.0390625
- pre_act: float32 [2, 2, 256, 24576], P('section', None, None, 'hid'), may hold values from -6 to 6
Outputs:
- grads: float32 [2, 2, 256, 6144], P('section', None, None, 'wid')
All inputs are finite; a program needn't handle non-finite values.
Results may differ from a plain program's by a relative error of at most 0.003.
Values may be sent and summed in bfloat16 or wider, within the bound.
A program may use at most 128 MiB of HBM per device.

v0:
```python
import jax
import jax.numpy as jnp
from jax import lax
from jax.sharding import PartitionSpec as P


def swapped(shard, axis, distance):
    return lax.ppermute(shard, axis, [(i, i ^ 1 << distance) for i in range(lax.axis_size(axis))])


def from_behind(block, axis, distance):
    devices = range(lax.axis_size(axis))
    route = [(i - distance, i) for i in devices if i - distance in devices]
    return lax.ppermute(block, axis, route)


def gelu_slope(pre):
    normal_cdf = 0.5 * (1.0 + jax.scipy.special.erf(pre * 0.7071067811865476))
    density = jnp.exp(-0.5 * pre * pre) * 0.3989422804014327
    return normal_cdf + pre * density


def local(grad_out, weight_in, weight_out, pre_act):
    section_pos = lax.axis_index("section")
    wid_pos = lax.axis_index("wid")
    is_down = section_pos == 0
    low_side = wid_pos % 2 == 0
    tile_in = weight_in[0]
    tile_out = weight_out[0]
    saved_pre = pre_act[0]
    quarter = tile_in.shape[0]
    hid_tile = tile_in.shape[1]
    half_tile = hid_tile // 2
    out_view = tile_out.reshape(half_tile, 2 * quarter)
    out_low = jnp.where(is_down, tile_out[:half_tile], out_view[:, :quarter])
    out_high = jnp.where(is_down, tile_out[half_tile:], out_view[:, quarter:])
    in_view = tile_in.reshape(2 * quarter, half_tile)
    in_low = jnp.where(is_down, tile_in[:, :half_tile], in_view[:quarter])
    in_high = jnp.where(is_down, tile_in[:, half_tile:], in_view[quarter:])
    batches = grad_out.shape[0]
    contract = (((1,), (1,)), ((), ()))
    results = []
    received = None
    for moment in range(batches + 1):
        fresh_grad = grad_out[min(moment, batches - 1)]
        batch_pick = jnp.clip(moment - section_pos, 0, batches - 1)
        pre_now = lax.dynamic_index_in_dim(saved_pre, batch_pick, 0, keepdims=False)
        if received is None:
            arrived = jnp.zeros_like(fresh_grad)
            partner = jnp.zeros(fresh_grad.shape, jnp.bfloat16)
        else:
            arrived = received
            partner = swapped(arrived.astype(jnp.bfloat16), "wid", 0)
        own_in = jnp.where(is_down, fresh_grad, arrived)
        fresh_low = fresh_grad.astype(jnp.bfloat16)
        arrived_low = arrived.astype(jnp.bfloat16)
        first_in = jnp.where(is_down, fresh_low, jnp.where(low_side, arrived_low, partner))
        second_in = jnp.where(is_down, fresh_low, jnp.where(low_side, partner, arrived_low))
        low_hidden = lax.dot_general(
            first_in, out_low, contract, preferred_element_type=jnp.float32
        )
        high_hidden = lax.dot_general(
            second_in, out_high, contract, preferred_element_type=jnp.float32
        )
        joined = low_hidden + high_hidden
        empty_slot = jnp.zeros_like(joined)
        up_part = jnp.concatenate(
            [jnp.where(low_side, joined, empty_slot), jnp.where(low_side, empty_slot, joined)],
            axis=1,
        )
        partial_hidden = jnp.where(
            is_down, jnp.concatenate([low_hidden, high_hidden], axis=1), up_part
        )
        hidden_grad = lax.psum(partial_hidden, "wid")
        hidden = (hidden_grad * gelu_slope(pre_now)).astype(jnp.bfloat16)
        own_slot = jnp.where(low_side, hidden[:, :half_tile], hidden[:, half_tile:])
        first_hidden = jnp.where(is_down, hidden[:, :half_tile], own_slot)
        second_hidden = jnp.where(is_down, hidden[:, half_tile:], own_slot)
        low_term = lax.dot_general(
            first_hidden, in_low, contract, preferred_element_type=jnp.float32
        )
        high_term = lax.dot_general(
            second_hidden, in_high, contract, preferred_element_type=jnp.float32
        )
        own_term = jnp.where(
            is_down, low_term + high_term, jnp.where(low_side, low_term, high_term)
        )
        send_term = jnp.where(
            is_down, jnp.zeros_like(low_term), jnp.where(low_side, high_term, low_term)
        )
        own_term, send_term = (own_term, send_term)
        partial_value = own_term + swapped(send_term, "wid", 0)
        result = own_in + lax.psum(partial_value, "hid")
        results.append(result)
        if moment < batches:
            received = from_behind(result, "section", 1)
    chosen = jnp.stack(
        [jnp.where(is_down, results[index_m], results[index_m + 1]) for index_m in range(batches)]
    )
    return chosen[None]


def solution(mesh):
    return jax.shard_map(
        local,
        mesh=mesh,
        in_specs=(
            P(None, None, "wid"),
            P("section", "wid", "hid"),
            P("section", "hid", "wid"),
            P("section", None, None, "hid"),
        ),
        out_specs=P("section", None, None, "wid"),
        check_vma=False,
    )
```

profile of v0, /device:TPU:65, one launch (start us, length us, event | category | flops | bytes accessed | tf_op | source)
XLA Modules:
  0.0 807.7 jit_solution(300099866139388536)
XLA Ops:
  6.5 8.0 reshape_squeeze.4
  14.5 4.1 slice_select_fusion.3
  20.8 0.8 broadcast_select_fusion.5
  21.6 1.3 maximum_select_fusion
  23.1 4.9 fusion.90
  28.0 4.7 slice.78
  32.7 4.8 slice.81
  37.6 6.5 slice_select_fusion.1
  44.1 31.1 %all-reduce.7.cloned.1.call-done = f32[256,1536]{1,0:T(8,128)} async-done(((f32[256,1536]{1,0:T(8,128)}), f32[256,1536]{1,0:T(8,128)}) %all-reduce.7.cloned.1.call-update) | async-done | bytes 1572880 | tf_op jit(solution)/shard_map/psum | solution.py:74
  75.1 2.7 fusion.5
  77.8 0.8 fusion.53
  78.6 0.8 copy-done.7
  80.4 35.2 %collective-permute-done = f32[256,1536]{1,0:T(8,128)S(1)} collective-permute-done((f32[256,1536]{1,0:T(8,128)S(1)}, f32[256,1536]{1,0:T(8,128)S(1)}, u32[]{:S(2)}, u32[]{:S(2)}) %collective-permute-start) | collective-permute-done | bytes 1572896 | tf_op jit(solution)/shard_map/ppermute | solution.py:8
  115.6 1.7 select_add_fusion.2
  117.3 122.0 %all-reduce.9.cloned.1.call-done = f32[256,1536]{1,0:T(8,128)} async-done(((f32[256,1536]{1,0:T(8,128)}), f32[256,1536]{1,0:T(8,128)}) %all-reduce.9.cloned.1.call-update) | async-done | bytes 1572880 | tf_op jit(solution)/shard_map/psum | solution.py:93
  239.3 1.6 bitcast_add_fusion
  241.0 1.6 collective-permute-start.1
  242.5 37.0 %collective-permute-done.1 = f32[256,1536]{1,0:T(8,128)S(1)} collective-permute-done((f32[256,1536]{1,0:T(8,128)S(1)}, f32[256,1536]{1,0:T(8,128)S(1)}, u32[]{:S(2)}, u32[]{:S(2)}) %collective-permute-start.1) | collective-permute-done | bytes 1572896 | tf_op jit(solution)/shard_map/ppermute | solution.py:14
  279.7 1.3 collective-permute-start.2
  281.0 16.0 %collective-permute-done.2 = bf16[256,1536]{1,0:T(8,128)(2,1)S(1)} collective-permute-done((bf16[256,1536]{1,0:T(8,128)(2,1)S(1)}, bf16[256,1536]{1,0:T(8,128)(2,1)S(1)}, u32[]{:S(2)}, u32[]{:S(2)}) %collective-permute-start.2) | collective-permute-done | bytes 786464 | tf_op jit(solution)/shard_map/ppermute | solution.py:8
  297.0 0.9 fusion.39
  298.7 1.0 broadcast_select_fusion.3
  299.6 1.4 maximum_select_fusion.1
  301.1 51.4 %all-reduce.11.cloned.1.call-done = f32[256,1536]{1,0:T(8,128)} async-done(((f32[256,1536]{1,0:T(8,128)}), f32[256,1536]{1,0:T(8,128)}) %all-reduce.11.cloned.1.call-update) | async-done | bytes 1572880 | tf_op jit(solution)/shard_map/psum | solution.py:74
  352.6 2.7 fusion.11
  356.1 0.8 copy-done.8
  356.9 0.8 select_select_fusion.1
  357.8 35.2 %collective-permute-done.3 = f32[256,1536]{1,0:T(8,128)S(1)} collective-permute-done((f32[256,1536]{1,0:T(8,128)S(1)}, f32[256,1536]{1,0:T(8,128)S(1)}, u32[]{:S(2)}, u32[]{:S(2)}) %collective-permute-start.3) | collective-permute-done | bytes 1572896 | tf_op jit(solution)/shard_map/ppermute | solution.py:8
  393.0 1.7 select_add_fusion.1
  395.0 121.9 %all-reduce.13.cloned.1.call-done = f32[256,1536]{1,0:T(8,128)} async-done(((f32[256,1536]{1,0:T(8,128)}), f32[256,1536]{1,0:T(8,128)}) %all-reduce.13.cloned.1.call-update) | async-done | bytes 1572880 | tf_op jit(solution)/shard_map/psum | solution.py:93
  516.9 3.7 select_bitcast_fusion
  520.6 1.5 collective-permute-start.4
  522.2 37.0 %collective-permute-done.4 = f32[256,1536]{1,0:T(8,128)S(1)} collective-permute-done((f32[256,1536]{1,0:T(8,128)S(1)}, f32[256,1536]{1,0:T(8,128)S(1)}, u32[]{:S(2)}, u32[]{:S(2)}) %collective-permute-start.4) | collective-permute-done | bytes 1572896 | tf_op jit(solution)/shard_map/ppermute | solution.py:14
  559.3 1.3 collective-permute-start.5
  560.6 16.0 %collective-permute-done.5 = bf16[256,1536]{1,0:T(8,128)(2,1)S(1)} collective-permute-done((bf16[256,1536]{1,0:T(8,128)(2,1)S(1)}, bf16[256,1536]{1,0:T(8,128)(2,1)S(1)}, u32[]{:S(2)}, u32[]{:S(2)}) %collective-permute-start.5) | collective-permute-done | bytes 786464 | tf_op jit(solution)/shard_map/ppermute | solution.py:8
  576.6 0.9 fusion.33
  578.3 0.9 broadcast_select_fusion.1
  579.2 1.4 maximum_select_fusion.2
  580.7 51.4 %all-reduce.15.cloned.1.call-done = f32[256,1536]{1,0:T(8,128)} async-done(((f32[256,1536]{1,0:T(8,128)}), f32[256,1536]{1,0:T(8,128)}) %all-reduce.15.cloned.1.call-update) | async-done | bytes 1572880 | tf_op jit(solution)/shard_map/psum | solution.py:74
  632.1 2.7 fusion.17
  634.8 0.8 fusion.57
  635.6 0.8 copy-done.9
  636.4 0.8 select_select_fusion
  637.4 35.2 %collective-permute-done.6 = f32[256,1536]{1,0:T(8,128)S(1)} collective-permute-done((f32[256,1536]{1,0:T(8,128)S(1)}, f32[256,1536]{1,0:T(8,128)S(1)}, u32[]{:S(2)}, u32[]{:S(2)}) %collective-permute-start.6) | collective-permute-done | bytes 1572896 | tf_op jit(solution)/shard_map/ppermute | solution.py:8
  672.5 1.7 select_add_fusion
  674.2 122.2 %all-reduce.17.cloned.1.call-done = f32[256,1536]{1,0:T(8,128)} async-done(((f32[256,1536]{1,0:T(8,128)}), f32[256,1536]{1,0:T(8,128)}) %all-reduce.17.cloned.1.call-update) | async-done | bytes 1572880 | tf_op jit(solution)/shard_map/psum | solution.py:93
  796.4 2.6 fusion.27
  799.0 1.9 maximum_bitcast_fusion
  (53 shorter events, 6.2 us)
Async XLA Ops:
  6.5 68.6 %all-reduce.7.cloned.1.call-start = ((), (), s32[]{:S(2)}) async-start(), calls=%async_computation | async-start | bytes 3145728 | tf_op jit(solution)/shard_map/psum | solution.py:74
  14.5 4.7 copy-start
  18.6 1.4 copy-start.4
  18.6 2.1 copy-start.1
  23.0 216.3 %all-reduce.9.cloned.1.call-start = ((), (), s32[]{:S(2)}) async-start(), calls=%async_computation.1 | async-start | bytes 3145728 | tf_op jit(solution)/shard_map/psum | solution.py:93
  75.1 2.7 copy-start.15
  77.8 1.7 copy-start.7
  80.3 35.3 %collective-permute-start = (f32[256,1536]{1,0:T(8,128)S(1)}, f32[256,1536]{1,0:T(8,128)S(1)}, u32[]{:S(2)}, u32[]{:S(2)}) collective-permute-start(f32[256,1536]{1,0:T(8,128)S(1)} %get-tuple-element.20), channel_id=1, source_target_pairs={{0,1},{1,0},{2,3},{3,2},{4,5},{5,4},{6,7},{7,6},{8,9},{9,8},{10,11... | collective-permute-start | bytes 4718600 | tf_op jit(solution)/shard_map/ppermute | solution.py:8
  117.2 235.3 %all-reduce.11.cloned.1.call-start = ((), (), s32[]{:S(2)}) async-start(), calls=%async_computation.2 | async-start | bytes 3145728 | tf_op jit(solution)/shard_map/psum | solution.py:74
  241.0 40.0 %copy-start.10 = (f32[256,1536]{1,0:T(8,128)}, f32[256,1536]{1,0:T(8,128)S(1)}, u32[]{:S(2)}) copy-start(f32[256,1536]{1,0:T(8,128)S(1)} %bitcast_add_fusion) | copy-start | bytes 4718596
  241.0 56.0 %copy-start.5 = (bf16[768,1536]{1,0:T(8,128)(2,1)S(1)}, bf16[768,1536]{1,0:T(8,128)(2,1)}, u32[]{:S(2)}) copy-start(bf16[768,1536]{1,0:T(8,128)(2,1)} %copy-done.4) | copy-start | bytes 7077892
  241.0 38.6 %collective-permute-start.1 = (f32[256,1536]{1,0:T(8,128)S(1)}, f32[256,1536]{1,0:T(8,128)S(1)}, u32[]{:S(2)}, u32[]{:S(2)}) collective-permute-start(f32[256,1536]{1,0:T(8,128)S(1)} %bitcast_add_fusion), channel_id=1, source_target_pairs={{0,64},{1,65},{2,66},{3,67},{4,68},{5,69},{6,70},{7,71},{8,72},{9,... | collective-permute-start | bytes 4718600 | tf_op jit(solution)/shard_map/ppermute | solution.py:14
  279.6 1.4 copy-start.12
  279.7 17.3 %collective-permute-start.2 = (bf16[256,1536]{1,0:T(8,128)(2,1)S(1)}, bf16[256,1536]{1,0:T(8,128)(2,1)S(1)}, u32[]{:S(2)}, u32[]{:S(2)}) collective-permute-start(bf16[256,1536]{1,0:T(8,128)(2,1)S(1)} %convert_element_type.30), channel_id=1, source_target_pairs={{0,1},{1,0},{2,3},{3,2},{4,5},{5,4},{6,7},{7,6},{8,9},{9,8},{10,11... | collective-permute-start | bytes 2359304 | tf_op jit(solution)/shard_map/ppermute | solution.py:8
  297.0 1.7 copy-start.2
  301.1 215.8 %all-reduce.13.cloned.1.call-start = ((), (), s32[]{:S(2)}) async-start(), calls=%async_computation.3 | async-start | bytes 3145728 | tf_op jit(solution)/shard_map/psum | solution.py:93
  352.6 2.7 copy-start.16
  355.2 1.7 copy-start.8
  357.7 35.3 %collective-permute-start.3 = (f32[256,1536]{1,0:T(8,128)S(1)}, f32[256,1536]{1,0:T(8,128)S(1)}, u32[]{:S(2)}, u32[]{:S(2)}) collective-permute-start(f32[256,1536]{1,0:T(8,128)S(1)} %get-tuple-element.23), channel_id=1, source_target_pairs={{0,1},{1,0},{2,3},{3,2},{4,5},{5,4},{6,7},{7,6},{8,9},{9,8},{10,11... | collective-permute-start | bytes 4718600 | tf_op jit(solution)/shard_map/ppermute | solution.py:8
  394.8 237.3 %all-reduce.15.cloned.1.call-start = ((), (), s32[]{:S(2)}) async-start(), calls=%async_computation.4 | async-start | bytes 3145728 | tf_op jit(solution)/shard_map/psum | solution.py:74
  520.6 56.9 %copy-start.13 = (f32[256,1536]{1,0:T(8,128)}, f32[256,1536]{1,0:T(8,128)S(1)}, u32[]{:S(2)}) copy-start(f32[256,1536]{1,0:T(8,128)S(1)} %get-tuple-element.6) | copy-start | bytes 4718596
  520.6 56.0 %copy-start.6 = (bf16[768,1536]{1,0:T(8,128)(2,1)S(1)}, bf16[768,1536]{1,0:T(8,128)(2,1)}, u32[]{:S(2)}) copy-start(bf16[768,1536]{1,0:T(8,128)(2,1)} %copy-done.4) | copy-start | bytes 7077892
  520.6 38.6 %collective-permute-start.4 = (f32[256,1536]{1,0:T(8,128)S(1)}, f32[256,1536]{1,0:T(8,128)S(1)}, u32[]{:S(2)}, u32[]{:S(2)}) collective-permute-start(f32[256,1536]{1,0:T(8,128)S(1)} %get-tuple-element.6), channel_id=1, source_target_pairs={{0,64},{1,65},{2,66},{3,67},{4,68},{5,69},{6,70},{7,71},{8,72},{9,... | collective-permute-start | bytes 4718600 | tf_op jit(solution)/shard_map/ppermute | solution.py:14
  559.2 1.4 copy-start.14
  559.3 17.3 %collective-permute-start.5 = (bf16[256,1536]{1,0:T(8,128)(2,1)S(1)}, bf16[256,1536]{1,0:T(8,128)(2,1)S(1)}, u32[]{:S(2)}, u32[]{:S(2)}) collective-permute-start(bf16[256,1536]{1,0:T(8,128)(2,1)S(1)} %convert_element_type.32), channel_id=1, source_target_pairs={{0,1},{1,0},{2,3},{3,2},{4,5},{5,4},{6,7},{7,6},{8,9},{9,8},{10,11... | collective-permute-start | bytes 2359304 | tf_op jit(solution)/shard_map/ppermute | solution.py:8
  576.6 1.7 copy-start.3
  580.7 215.7 %all-reduce.17.cloned.1.call-start = ((), (), s32[]{:S(2)}) async-start(), calls=%async_computation.5 | async-start | bytes 3145728 | tf_op jit(solution)/shard_map/psum | solution.py:93
  632.1 2.7 copy-start.17
  634.8 1.7 copy-start.9
  637.3 35.3 %collective-permute-start.6 = (f32[256,1536]{1,0:T(8,128)S(1)}, f32[256,1536]{1,0:T(8,128)S(1)}, u32[]{:S(2)}, u32[]{:S(2)}) collective-permute-start(f32[256,1536]{1,0:T(8,128)S(1)} %get-tuple-element.26), channel_id=1, source_target_pairs={{0,1},{1,0},{2,3},{3,2},{4,5},{5,4},{6,7},{7,6},{8,9},{9,8},{10,11... | collective-permute-start | bytes 4718600 | tf_op jit(solution)/shard_map/ppermute | solution.py:8
  796.4 2.6 copy-start.11
Sparse Core Ops, SparseCore 0:
  23.1 51.9 all-reduce.6
  117.4 121.9 all-reduce.8
  301.2 51.3 all-reduce.10
  394.9 121.9 all-reduce.12
  580.8 51.2 all-reduce.14
  674.3 122.0 all-reduce.16
where the time goes:
time: 810 us; the launch traced here: 808 us
  waiting for transfers between devices  712 us (88%)
  other arithmetic  37.9 us (5%)
  local copies, waits for them, and re-layouts  27.8 us (3%)
  between operations  13.8 us (2%)
  matrix products  10.3 us (1%)
    psum x3, waiting for transfers between devices, local(): result = own_in + lax.psum(partial_value, 'hid')  366 us
    ppermute x5, waiting for transfers between devices, swapped(): lax.ppermute(shard, axis, [(i, i ^ 1 << distance) for i in range(lax.axis...  138 us
    psum x3, waiting for transfers between devices, local(): hidden_grad = lax.psum(partial_hidden, 'wid')  134 us
    ppermute x2, waiting for transfers between devices, from_behind(): return lax.ppermute(block, axis, route)  74.1 us
  transfers between devices with their start and end apart: 13, of which 13 were waited for; matrix products, arithmetic and copies ran while one was open for 3% of the time, Pallas kernels for 0%

commit v1 on v0

v1 whole, which is shorter than its diff:
```python
import jax
import jax.numpy as jnp
from jax import lax
from jax.experimental import pallas as pl
from jax.experimental.pallas import tpu as pltpu
from jax.sharding import PartitionSpec as P

F32 = jnp.float32
BF16 = jnp.bfloat16
MESH = pl.DeviceIdType.MESH
N_REMOTE = 96
N_LOCAL = 24
NT = (((1,), (1,)), ((), ()))


def gelu_slope(pre):
    normal_cdf = 0.5 * (1.0 + lax.erf(pre * 0.7071067811865476))
    density = jnp.exp(-0.5 * pre * pre) * 0.3989422804014327
    return normal_cdf + pre * density


def dot_nt(a, b):
    return lax.dot_general(a, b, NT, preferred_element_type=F32)


def kernel(
    grad, win, wout, pre, out,
    v_raw, w_raw, v_nat, w_nat, stripe, gbuf, glow, prev, pa, r1, r2, hid, sb, rl, rp, pb, rc,
    xs, xr1, xr2, xsum, yr, ys, zr, bs, ob,
    send_sem, recv_sem, local_sem,
):
    s = lax.axis_index("section")
    h = lax.axis_index("hid")
    w = lax.axis_index("wid")
    x = lax.div(h, 4)
    zl = lax.rem(lax.div(h, 2), 2)
    core = lax.rem(h, 2)
    c = lax.div(w, 2)
    b = lax.rem(w, 2)
    zc = zl + s - 2 * zl * s
    batches, tok, tile = grad.shape
    half, fourth = tile // 2, tile // 4
    th, tq = tok // 2, tok // 4
    te = tq // 2

    def device(dx=0, dw=0, flip_core=False, flip_z=False, flip_s=False, flip_w=False):
        nx = lax.rem(x + dx + 4, 4) if dx else x
        nz = 1 - zl if flip_z else zl
        nc = 1 - core if flip_core else core
        nw = lax.rem(w + dw + 4, 4) if dw else w
        if flip_w:
            nw = w + 1 - 2 * b
        return {"section": 1 - s if flip_s else s, "hid": nx * 4 + nz * 2 + nc, "wid": nw}

    right, left = device(dx=1), device(dx=-1)
    up, down = device(dw=1), device(dw=-1)
    mate = device(flip_core=True)
    zmate = device(flip_z=True)
    cross = device(flip_s=True, flip_z=True)
    wmate = device(flip_w=True)

    keys = {}

    def remote(key, src, dst, to):
        index = keys.setdefault(key, len(keys))
        return pltpu.make_async_remote_copy(
            src_ref=src, dst_ref=dst, send_sem=send_sem.at[index], recv_sem=recv_sem.at[index],
            device_id=to, device_id_type=MESH,
        )

    local_keys = {}

    def local(key, src, dst):
        index = local_keys.setdefault(key, len(local_keys))
        return pltpu.make_async_copy(src, dst, local_sem.at[index])

    def of4(i):
        return lax.rem(i + 4, 4)

    def cols(start, size):
        return pl.ds(pl.multiple_of(start, size), size)

    started = []

    def send(copy):
        copy.start()
        started.append(copy)
        return copy

    pre_col = jnp.where(s == 0, fourth * w, half * b + fourth * c)
    pre_loads = [
        local(("pre", m), pre.at[0, m, :, cols(pre_col, fourth)], prev.at[m]) for m in range(batches)
    ]
    v_loads = [
        local(("v", r), wout.at[0, cols(fourth * of4(w + r), fourth), :],
              v_raw.at[cols(fourth * of4(w + r), fourth), :])
        for r in (2, 1, 3, 0)
    ]
    w_load = local("w", win.at[0], w_raw)
    g_loads = [local(("g", m), grad.at[m], gbuf.at[m]) for m in range(batches)]

    @pl.when(s == 0)
    def _():
        g_loads[0].start()

    for load in v_loads:
        load.start()
    for load in pre_loads:
        load.start()
    w_load.start()

    @pl.when(s == 0)
    def _():
        for load in g_loads[1:]:
            load.start()

    barrier = pltpu.get_barrier_semaphore()
    for peer in (right, left, up, down, mate, zmate, cross):
        pl.semaphore_signal(barrier, inc=1, device_id=peer, device_id_type=MESH)
    pl.semaphore_wait(barrier, 7)

    def slope_stage(m):
        pre_loads[m].wait()

        @pl.loop(0, 8)
        def _(i):
            rows = cols(i * (tok // 8), tok // 8)
            prev[m, rows, :] = gelu_slope(prev[m, rows, :])


    def core_send(m, q):
        return send(remote(("core", m, q), pb.at[m, q, 1 - core], rc.at[m, q], mate))

    def x_rows(r):
        return cols(tq * of4(x + r), tq)

    def chip_sum(m, q, r):
        rows = x_rows(r)
        return pb[m, q, core, rows, :] + rc[m, q, rows, :]

    def x_first(m, nq):
        for q in range(nq):
            xs[m, 0, q] = chip_sum(m, q, 2).astype(BF16)
        one = remote(("x1r", m), xs.at[m, 0, pl.ds(0, nq), pl.ds(0, te)], xr1.at[m, 0, pl.ds(0, nq)], right)
        two = remote(("x1l", m), xs.at[m, 0, pl.ds(0, nq), pl.ds(te, te)], xr1.at[m, 1, pl.ds(0, nq)], left)
        return send(one), send(two)

    def x_second(m, nq, first):
        result = []
        for side, (copy, r, to) in enumerate(((first[0], 1, right), (first[1], 3, left))):
            copy.wait_recv()
            lo = te * side
            for q in range(nq):
                total = chip_sum(m, q, r)
                xs[m, 1 + side, q] = total.astype(BF16)
                part = total[lo : lo + te] + xr1[m, side, q].astype(F32)
                xs[m, 1 + side, q, lo : lo + te] = part.astype(BF16)
            copy = remote(
                ("x2", m, side), xs.at[m, 1 + side, pl.ds(0, nq)], xr2.at[m, side, pl.ds(0, nq)], to
            )
            result.append(send(copy))
        return result

    def x_last(m, nq, second):
        for copy in second:
            copy.wait_recv()
        for q in range(nq):
            xsum[m, q] = chip_sum(m, q, 0) + xr2[m, 0, q].astype(F32) + xr2[m, 1, q].astype(F32)

    def z_stage(m):
        copy = send(remote(("z", m), ys.at[m, :, cols(fourth * (1 - zc), fourth)], zr.at[m], zmate))
        copy.wait_recv()
        return ys[m, :, cols(fourth * zc, fourth)] + zr[m]


    def shard_of(ref, m):
        return ref.at[m, core, cols(tq * x, tq), cols(fourth * zc, fourth)]

    def out_stage(m):
        first = send(remote(("oz", m), shard_of(ob, m), shard_of(ob, m), zmate))
        first.wait_recv()
        own = ob.at[m, core, cols(tq * x, tq)]
        to_right = send(remote(("ox1r", m), own, own, right))
        to_left = send(remote(("ox1l", m), own, own, left))
        to_right.wait_recv()
        piece = ob.at[m, core, cols(tq * of4(x - 1), te)]
        on_right = send(remote(("ox2r", m), piece, piece, right))
        to_left.wait_recv()
        piece = ob.at[m, core, cols(tq * of4(x + 1) + te, te)]
        on_left = send(remote(("ox2l", m), piece, piece, left))
        on_right.wait_recv()
        on_left.wait_recv()
        column = ob.at[m, core]
        last = send(remote(("oc", m), column, column, mate))
        mine = local(("om", m), column, out.at[0, m, :, cols(half * core, half)])
        mine.start()
        last.wait_recv()
        other = local(("oo", m), ob.at[m, 1 - core], out.at[0, m, :, cols(half * (1 - core), half)])
        other.start()
        return mine, other


    def down_hidden(m):
        g_loads[m].wait()
        for k in range(2):
            glow[m, 0, k] = gbuf[m, :, k * half : (k + 1) * half].astype(BF16)

        def partial(r):
            if m == 0:
                v_loads[(2, 1, 3, 0).index(r)].wait()
            rows = cols(fourth * of4(w + r), fourth)
            pa[m, r] = dot_nt(glow[m, 0, 0], v_raw[rows, :half]) + dot_nt(glow[m, 0, 1], v_raw[rows, half:])

        partial(2)
        one = send(remote(("a1u", m), pa.at[m, 2, pl.ds(0, th)], r1.at[m, 0], up))
        two = send(remote(("a1d", m), pa.at[m, 2, pl.ds(th, th)], r1.at[m, 1], down))
        partial(1)
        partial(3)
        one.wait_recv()
        pa[m, 1, :th] += r1[m, 0]
        three = send(remote(("a2u", m), pa.at[m, 1], r2.at[m, 0], up))
        two.wait_recv()
        pa[m, 3, th:] += r1[m, 1]
        four = send(remote(("a2d", m), pa.at[m, 3], r2.at[m, 1], down))
        partial(0)
        slope_stage(m)
        three.wait_recv()
        four.wait_recv()
        mine = cols(fourth * w, fourth)
        total = pa[m, 0] + r2[m, 0] + r2[m, 1]
        hid[m, :, mine] = (total * prev[m]).astype(BF16)
        own = hid.at[m, :, mine]
        to_up = send(remote(("h1u", m), own, own, up))
        to_down = send(remote(("h1d", m), own, own, down))
        to_up.wait_recv()
        piece = hid.at[m, pl.ds(0, th), cols(fourth * of4(w - 1), fourth)]
        on_up = send(remote(("h2u", m), piece, piece, up))
        to_down.wait_recv()
        piece = hid.at[m, pl.ds(th, th), cols(fourth * of4(w + 1), fourth)]
        on_down = send(remote(("h2d", m), piece, piece, down))
        on_up.wait_recv()
        on_down.wait_recv()

    def down_back(m):
        if m == 0:
            w_load.wait()

        def product(k):
            @pl.loop(0, 3)
            def _(n):
                rows = cols(half * k + (half // 3) * n, half // 3)
                pb[m, 0, k, :, cols((half // 3) * n, half // 3)] = dot_nt(hid[m], w_raw[rows, :])

        product(1 - core)
        copy = core_send(m, 0)
        product(core)
        copy.wait_recv()
        x_last(m, 1, x_second(m, 1, x_first(m, 1)))
        ys[m] = xsum[m, 0]
        total = z_stage(m)
        rows, columns = cols(tq * x, tq), cols(fourth * zc, fourth)
        ob[m, core, rows, columns] = total + gbuf[m, rows, cols(half * core + fourth * zc, fourth)]
        send(cross_copy(m))

    def cross_copy(m):
        return remote(("cross", m), shard_of(ob, m), bs.at[m], cross)

    @pl.when(s == 0)
    def _():
        for m in range(batches):
            down_hidden(m)
            down_back(m)
        last = []
        for m in range(batches):
            last += out_stage(m)
        for copy in last:
            copy.wait()
        for copy in started:
            copy.wait_send()

    started.clear()


    def up_weights():
        for load in v_loads:
            load.wait()

        @pl.loop(0, tile // 128)
        def _(i):
            columns = cols(128 * i, 128)
            stripe[:tile, :] = v_raw[:, columns].astype(F32)
            for q in range(2):
                v_nat[q, :, columns] = stripe[pl.ds(q, half, stride=2), :].astype(BF16)

        w_load.wait()

        @pl.loop(0, half // 128)
        def _(i):
            for q in range(2):
                stripe[pl.ds(q, tile, stride=2), :] = w_raw[:, cols(half * q + 128 * i, 128)].astype(F32)
            w_nat[:, cols(128 * i, 128)] = stripe[...].astype(BF16)

    def up_gather(m):
        cross_copy(m).wait_recv()
        rows, columns = cols(tq * x, tq), cols(fourth * zc, fourth)
        glow[m, b, core, rows, columns] = bs[m].astype(BF16)
        own = glow.at[m, b, core, rows, columns]
        copy = send(remote(("gw", m), own, own, wmate))
        copy.wait_recv()
        own = glow.at[m, :, core, rows, columns]
        copy = send(remote(("gz", m), own, own, zmate))
        copy.wait_recv()
        own = glow.at[m, :, core, rows]
        to_right = send(remote(("gx1r", m), own, own, right))
        to_left = send(remote(("gx1l", m), own, own, left))
        to_right.wait_recv()
        piece = glow.at[m, :, core, cols(tq * of4(x - 1), te)]
        on_right = send(remote(("gx2r", m), piece, piece, right))
        to_left.wait_recv()
        piece = glow.at[m, :, core, cols(tq * of4(x + 1) + te, te)]
        on_left = send(remote(("gx2l", m), piece, piece, left))
        on_right.wait_recv()
        on_left.wait_recv()
        column = glow.at[m, :, core]
        copy = send(remote(("gc", m), column, column, mate))
        copy.wait_recv()

    def opposite(name, m, src, dst, relays):
        one = send(remote((name, "1u", m), src.at[pl.ds(0, th)], relays.at[0], up))
        two = send(remote((name, "1d", m), src.at[pl.ds(th, th)], relays.at[1], down))
        one.wait_recv()
        three = send(remote((name, "2u", m), relays.at[0], dst(0, w - 1), up))
        two.wait_recv()
        four = send(remote((name, "2d", m), relays.at[1], dst(1, w + 1), down))
        three.wait_recv()
        four.wait_recv()

    def up_hidden(m):
        def partial(part):
            rows = cols(fourth * part, fourth)
            total = None
            for q in range(2):
                for k in range(2):
                    term = dot_nt(glow[m, q, k], v_nat[q, rows, k * half : (k + 1) * half])
                    total = term if total is None else total + term
            return total

        sb[m] = partial(1 - c).astype(BF16)
        pa[m, 0] = partial(c)
        opposite("p", m, sb.at[m], lambda side, _: rp.at[m, pl.ds(th * side, th)], rl.at[m, 0])
        mine = cols(fourth * c, fourth)
        total = pa[m, 0] + rp[m].astype(F32)
        hid[m, :, mine] = (total * prev[m]).astype(BF16)
        opposite(
            "h", m, hid.at[m, :, mine],
            lambda side, i: hid.at[m, pl.ds(th * side, th), cols(fourth * lax.div(of4(i), 2), fourth)],
            rl.at[m, 1],
        )

    def up_back(m):
        def product(q, k):
            @pl.loop(0, 3)
            def _(n):
                rows = cols(tile * q + half * k + (half // 3) * n, half // 3)
                pb[m, q, k, :, cols((half // 3) * n, half // 3)] = dot_nt(hid[m, :, :half], w_nat[rows, :])

        copies = []
        for q in range(2):
            product(q, 1 - core)
            copies.append(core_send(m, q))
        for q in range(2):
            product(q, core)
        for copy in copies:
            copy.wait_recv()
        x_last(m, 2, x_second(m, 2, x_first(m, 2)))
        copy = send(remote(("y", m), xsum.at[m, 1 - b], yr.at[m], wmate))
        copy.wait_recv()
        ys[m] = xsum[m, b] + yr[m]
        total = z_stage(m)
        rows, columns = cols(tq * x, tq), cols(fourth * zc, fourth)
        ob[m, core, rows, columns] = total + bs[m]

    @pl.when(s == 1)
    def _():
        up_weights()
        for m in range(batches):
            slope_stage(m)
        last = []
        for m in range(batches):
            up_gather(m)
            up_hidden(m)
            up_back(m)
            last += out_stage(m)
        for copy in last:
            copy.wait()
        for copy in started:
            copy.wait_send()


def local(grad_out, weight_in, weight_out, pre_act):
    batches, tok, tile = grad_out.shape
    half, fourth = tile // 2, tile // 4
    th, tq = tok // 2, tok // 4
    vmem = pltpu.VMEM
    scratch = [
        vmem((tile, tile), BF16),
        vmem((tile, tile), BF16),
        vmem((2, half, tile), BF16),
        vmem((2 * tile, half), BF16),
        vmem((2 * tile, 128), F32),
        vmem((batches, tok, tile), F32),
        vmem((batches, 2, 2, tok, half), BF16),
        vmem((batches, tok, fourth), F32),
        vmem((batches, 4, tok, fourth), F32),
        vmem((batches, 2, th, fourth), F32),
        vmem((batches, 2, tok, fourth), F32),
        vmem((batches, tok, tile), BF16),
        vmem((batches, tok, fourth), BF16),
        vmem((batches, 2, 2, th, fourth), BF16),
        vmem((batches, tok, fourth), BF16),
        vmem((batches, 2, 2, tok, half), F32),
        vmem((batches, 2, tok, half), F32),
        vmem((batches, 3, 2, tq, half), BF16),
        vmem((batches, 2, 2, tq // 2, half), BF16),
        vmem((batches, 2, 2, tq, half), BF16),
        vmem((batches, 2, tq, half), F32),
        vmem((batches, tq, half), F32),
        vmem((batches, tq, half), F32),
        vmem((batches, tq, fourth), F32),
        vmem((batches, tq, fourth), F32),
        vmem((batches, 2, tok, half), F32),
        pltpu.SemaphoreType.DMA((N_REMOTE,)),
        pltpu.SemaphoreType.DMA((N_REMOTE,)),
        pltpu.SemaphoreType.DMA((N_LOCAL,)),
    ]
    anywhere = pl.BlockSpec(memory_space=pl.ANY)
    return pl.pallas_call(
        kernel,
        out_shape=jax.ShapeDtypeStruct((1, batches, tok, tile), F32),
        in_specs=[anywhere] * 4,
        out_specs=anywhere,
        scratch_shapes=scratch,
        compiler_params=pltpu.CompilerParams(
            collective_id=0, has_side_effects=True, vmem_limit_bytes=67_000_000
        ),
    )(grad_out, weight_in, weight_out, pre_act)


def solution(mesh):
    return jax.shard_map(
        local,
        mesh=mesh,
        in_specs=(
            P(None, None, "wid"),
            P("section", "wid", "hid"),
            P("section", "hid", "wid"),
            P("section", None, None, "hid"),
        ),
        out_specs=P("section", None, None, "wid"),
        check_vma=False,
    )
```

time: 810 us -> 210 us (0.26)
  waiting for transfers between devices: 712 us -> 0 us
  Pallas kernels: 0 us -> 204 us
  other arithmetic: 37.9 us -> 0 us
  local copies, waits for them, and re-layouts: 27.8 us -> 3.76 us
  between operations: 13.8 us -> 0.01 us
  matrix products: 10.3 us -> 0 us
    psum x6 -> x0, waiting for transfers between devices: 500 us -> none  [the longest x3 366 us: local(): result = own_in + lax.psum(partial_value, 'hid')]
    ppermute x7 -> x0, waiting for transfers between devices: 212 us -> none  [the longest x5 138 us: swapped(): lax.ppermute(shard, axis, [(i, i ^ 1 << distance) for i in range(lax.axis...]
    pallas_call x0 -> x1, Pallas kernels: none -> 204 us  [local(): pl.pallas_call(kernel, out_shape=jax.ShapeDtypeStruct((1, batches, tok, t...]
    select_n x5 -> x0, other arithmetic: 14.8 us -> none  [the longest x1 6.52 us: local(): in_low = jnp.where(is_down, tile_in[:, :half_tile], in_view[:quarter])]
    slice x3 -> x0, local copies, waits for them, and re-layouts: 14.5 us -> none  [the longest x2 9.64 us: local(): in_low = jnp.where(is_down, tile_in[:, :half_tile], in_view[:quarter])]
    dot_general x12 -> x0, matrix products: 10.3 us -> none  [the longest x3 2.75 us: local(): lax.dot_general(first_in, out_low, contract, preferred_element_type=jnp.f...]
    convert_element_type x5 -> x0, other arithmetic: 8.17 us -> none  [the longest x3 8.01 us: local(): hidden = (hidden_grad * gelu_slope(pre_now)).astype(jnp.bfloat16)]
  transfers between devices with their start and end apart: 13 -> 0, of which waited for: 13 -> 0; matrix products, arithmetic and copies ran while one was open for 3% -> 0% of each run, Pallas kernels for 0% -> 0%
where the time goes in v1:
time: 210 us; the launch traced here: 208 us
  Pallas kernels  204 us (97%)
  local copies, waits for them, and re-layouts  3.76 us (2%)
    pallas_call x1, Pallas kernels, local(): pl.pallas_call(kernel, out_shape=jax.ShapeDtypeStruct((1, batches, tok, t...  204 us

profile of v1, /device:TPU:65, one launch (start us, length us, event | category | flops | bytes accessed | tf_op | source)
XLA Modules:
  0.0 208.0 jit_solution(6084573226856022090)
XLA Ops:
  0.0 204.3 %shard_map.46 = f32[1,2,256,1536]{3,2,1,0:T(8,128)} custom-call(f32[2,256,1536]{2,1,0:T(8,128)} %grad.1, bf16[1,1536,1536]{2,1,0:T(8,128)(2,1)} %win.1, bf16[1,1536,1536]{2,1,0:T(8,128)(2,1)} %wout.1, f32[1,2,256,1536]{3,2,1,0:T(8,128)} %pre.1), custom_call_target="tpu_custom_call" | custom-call | tf_op jit(solution)/shard_map/pallas_call | solution.py:437
  204.3 3.8 %copy.6 = f32[1,2,256,1536]{3,2,1,0:T(8,128)} copy(f32[1,2,256,1536]{3,2,1,0:T(8,128)} %shard_map.46) | data formatting | bytes 6291456

commit v2 on v1

v2 whole, which is shorter than its diff:
```python
import jax
import jax.numpy as jnp
from jax import lax
from jax.experimental import pallas as pl
from jax.experimental.pallas import tpu as pltpu
from jax.sharding import PartitionSpec as P

F32 = jnp.float32
BF16 = jnp.bfloat16
MESH = pl.DeviceIdType.MESH
N_REMOTE = 240
N_LOCAL = 32
SPLIT = 2
START_DOWN = (0, 3, 5, 7)
START_UP = (0, 2, 4, 6)
NT = (((1,), (1,)), ((), ()))


def gelu_slope(pre):
    normal_cdf = 0.5 * (1.0 + lax.erf(pre * 0.7071067811865476))
    density = jnp.exp(-0.5 * pre * pre) * 0.3989422804014327
    return normal_cdf + pre * density


def dot_nt(a, b):
    return lax.dot_general(a, b, NT, preferred_element_type=F32)


def kernel(
    grad, win, wout, pre, out,
    v_raw, w_raw, v_nat, w_nat, stripe, gbuf, glow, gs, prev, pa, r1, r2, hid, pf, sb, rl, rp, pb, rc,
    xs, xr1, xr2, xsum, zr, bs, ob,
    send_sem, recv_sem, local_sem,
):
    s = lax.axis_index("section")
    h = lax.axis_index("hid")
    w = lax.axis_index("wid")
    x = lax.div(h, 4)
    zl = lax.rem(lax.div(h, 2), 2)
    core = lax.rem(h, 2)
    c = lax.div(w, 2)
    b = lax.rem(w, 2)
    zc = zl + s - 2 * zl * s
    tile = grad.shape[2]
    chunks, tok = pb.shape[0], pb.shape[3]
    half, fourth = tile // 2, tile // 4
    th, tq = tok // 2, tok // 4
    te = tq // 2

    def device(dx=0, dw=0, flip_core=False, flip_z=False, flip_s=False, flip_w=False):
        nx = lax.rem(x + dx + 4, 4) if dx else x
        nz = 1 - zl if flip_z else zl
        nc = 1 - core if flip_core else core
        nw = lax.rem(w + dw + 4, 4) if dw else w
        if flip_w:
            nw = w + 1 - 2 * b
        return {"section": 1 - s if flip_s else s, "hid": nx * 4 + nz * 2 + nc, "wid": nw}

    right, left = device(dx=1), device(dx=-1)
    up, down = device(dw=1), device(dw=-1)
    mate = device(flip_core=True)
    zmate = device(flip_z=True)
    wmate = device(flip_w=True)
    corner = device(flip_w=True, flip_z=True)
    cross = device(flip_s=True, flip_z=True)
    beyond = [
        device(flip_s=True), device(flip_s=True, flip_w=True), device(flip_s=True, flip_z=True, flip_w=True)
    ]

    keys = {}

    def remote(key, src, dst, to):
        index = keys.setdefault(key, len(keys))
        return pltpu.make_async_remote_copy(
            src_ref=src, dst_ref=dst, send_sem=send_sem.at[index], recv_sem=recv_sem.at[index],
            device_id=to, device_id_type=MESH,
        )

    local_keys = {}

    def local(key, src, dst):
        index = local_keys.setdefault(key, len(local_keys))
        return pltpu.make_async_copy(src, dst, local_sem.at[index])

    def of4(i):
        return lax.rem(i + 4, 4)

    def cols(start, size):
        return pl.ds(pl.multiple_of(start, size), size)

    started = []

    def send(copy):
        copy.start()
        started.append(copy)
        return copy


    def span(m):
        return m // SPLIT, pl.ds(tok * (m % SPLIT), tok)

    pre_down = [
        local(("pre", m), pre.at[(0, *span(m), cols(fourth * w, fourth))], prev.at[m, :, pl.ds(0, fourth)])
        for m in range(chunks)
    ]
    pre_up = [
        local(("pre", m), pre.at[(0, *span(m), cols(half * b, half))], prev.at[m]) for m in range(chunks)
    ]
    v_loads = [
        local(("v", r), wout.at[0, cols(fourth * of4(w + r), fourth), :],
              v_raw.at[cols(fourth * of4(w + r), fourth), :])
        for r in (2, 1, 3, 0)
    ]
    w_load = local("w", win.at[0], w_raw)
    g_loads = [local(("g", m), grad.at[span(m)], gbuf.at[m]) for m in range(chunks)]

    @pl.when(s == 0)
    def _():
        g_loads[0].start()

    for load in v_loads:
        load.start()
    w_load.start()

    @pl.when(s == 0)
    def _():
        for load in (*pre_down, *g_loads[1:]):
            load.start()

    @pl.when(s == 1)
    def _():
        for load in pre_up:
            load.start()

    barrier = pltpu.get_barrier_semaphore()
    peers = [right, left, up, down, mate, zmate, corner, cross, *beyond]
    for peer in peers:
        pl.semaphore_signal(barrier, inc=1, device_id=peer, device_id_type=MESH)
    pl.semaphore_wait(barrier, len(peers))

    def slope_stage(m, width):
        @pl.loop(0, 4)
        def _(i):
            rows = cols(i * (tok // 4), tok // 4)
            prev[m, rows, :width] = gelu_slope(prev[m, rows, :width])


    def core_send(m, q):
        return send(remote(("core", m, q), pb.at[m, q, 1 - core], rc.at[m, q], mate))

    def x_rows(r):
        return cols(tq * of4(x + r), tq)

    def chip_sum(m, q, r):
        rows = x_rows(r)
        return pb[m, q, core, rows, :] + rc[m, q, rows, :]

    def x_first(m, nq):
        for q in range(nq):
            xs[m, 0, q] = chip_sum(m, q, 2).astype(BF16)
        one = remote(("x1r", m), xs.at[m, 0, pl.ds(0, nq), pl.ds(0, te)], xr1.at[m, 0, pl.ds(0, nq)], right)
        two = remote(("x1l", m), xs.at[m, 0, pl.ds(0, nq), pl.ds(te, te)], xr1.at[m, 1, pl.ds(0, nq)], left)
        return send(one), send(two)

    def x_second(m, nq, first):
        result = []
        for side, (copy, r, to) in enumerate(((first[0], 1, right), (first[1], 3, left))):
            copy.wait_recv()
            lo = te * side
            for q in range(nq):
                total = chip_sum(m, q, r)
                xs[m, 1 + side, q] = total.astype(BF16)
                part = total[lo : lo + te] + xr1[m, side, q].astype(F32)
                xs[m, 1 + side, q, lo : lo + te] = part.astype(BF16)
            copy = remote(
                ("x2", m, side), xs.at[m, 1 + side, pl.ds(0, nq)], xr2.at[m, side, pl.ds(0, nq)], to
            )
            result.append(send(copy))
        return result

    def x_last(m, nq, second):
        for copy in second:
            copy.wait_recv()
        for q in range(nq):
            xsum[m, q] = chip_sum(m, q, 0) + xr2[m, 0, q].astype(F32) + xr2[m, 1, q].astype(F32)


    last = []

    def shard_of(ref, m):
        return ref.at[m, core, cols(tq * x, tq), cols(fourth * zc, fourth)]

    def ring_gather(name, m, block):
        own = block(tq * x, tq)
        to_right = send(remote((name, "1r", m), own, own, right))
        to_left = send(remote((name, "1l", m), own, own, left))
        copies = [send(remote((name, "c0", m), own, own, mate))]
        yield
        to_right.wait_recv()
        piece = block(tq * of4(x - 1), te)
        on_right = send(remote((name, "2r", m), piece, piece, right))
        to_left.wait_recv()
        piece = block(tq * of4(x + 1) + te, te)
        on_left = send(remote((name, "2l", m), piece, piece, left))
        for i in (1, 3):
            piece = block(tq * of4(x + i), tq)
            copies.append(send(remote((name, "c", i, m), piece, piece, mate)))
        yield
        on_right.wait_recv()
        on_left.wait_recv()
        piece = block(tq * of4(x + 2), tq)
        copies.append(send(remote((name, "c2", m), piece, piece, mate)))
        yield copies

    def spread(m):
        first = send(remote(("oz", m), shard_of(ob, m), shard_of(ob, m), zmate))
        yield
        first.wait_recv()
        for copies in ring_gather("o", m, lambda start, size: ob.at[m, core, cols(start, size)]):
            if copies is None:
                yield
        mine = local(("om", m), ob.at[m, core], out.at[(0, *span(m), cols(half * core, half))])
        mine.start()
        last.append(mine)
        yield
        for copy in copies:
            copy.wait_recv()
        other = local(("oo", m), ob.at[m, 1 - core], out.at[(0, *span(m), cols(half * (1 - core), half))])
        other.start()
        last.append(other)

    def interleave(chain, start):
        steps = [chain(m) for m in range(chunks)]
        turn = 0
        alive = set(range(chunks))
        while alive:
            for m in sorted(alive):
                if turn >= start[m] and next(steps[m], alive) is alive:
                    alive.discard(m)
            turn += 1
        for copy in last:
            copy.wait()
        for copy in started:
            copy.wait_send()
        last.clear()
        started.clear()


    def down_chain(m):
        g_loads[m].wait()
        for k in range(2):
            glow[m, 0, k] = gbuf[m, :, k * half : (k + 1) * half].astype(BF16)

        def partial(r):
            if m == 0:
                v_loads[(2, 1, 3, 0).index(r)].wait()
            rows = cols(fourth * of4(w + r), fourth)
            pa[m, r] = dot_nt(glow[m, 0, 0], v_raw[rows, :half]) + dot_nt(glow[m, 0, 1], v_raw[rows, half:])

        partial(2)
        one = send(remote(("a1u", m), pa.at[m, 2, pl.ds(0, th)], r1.at[m, 0], up))
        two = send(remote(("a1d", m), pa.at[m, 2, pl.ds(th, th)], r1.at[m, 1], down))
        partial(1)
        partial(3)
        yield
        one.wait_recv()
        pa[m, 1, :th] += r1[m, 0]
        three = send(remote(("a2u", m), pa.at[m, 1], r2.at[m, 0], up))
        two.wait_recv()
        pa[m, 3, th:] += r1[m, 1]
        four = send(remote(("a2d", m), pa.at[m, 3], r2.at[m, 1], down))
        partial(0)
        pre_down[m].wait()
        slope_stage(m, fourth)
        yield
        three.wait_recv()
        four.wait_recv()
        mine = cols(fourth * w, fourth)
        total = pa[m, 0] + r2[m, 0] + r2[m, 1]
        hid[m, :, mine] = (total * prev[m, :, :fourth]).astype(BF16)
        own = hid.at[m, :, mine]
        to_up = send(remote(("h1u", m), own, own, up))
        to_down = send(remote(("h1d", m), own, own, down))
        yield
        to_up.wait_recv()
        piece = hid.at[m, pl.ds(0, th), cols(fourth * of4(w - 1), fourth)]
        on_up = send(remote(("h2u", m), piece, piece, up))
        to_down.wait_recv()
        piece = hid.at[m, pl.ds(th, th), cols(fourth * of4(w + 1), fourth)]
        on_down = send(remote(("h2d", m), piece, piece, down))
        yield
        on_up.wait_recv()
        on_down.wait_recv()
        if m == 0:
            w_load.wait()

        def product(k):
            @pl.loop(0, 3)
            def _(n):
                rows = cols(half * k + (half // 3) * n, half // 3)
                pb[m, 0, k, :, cols((half // 3) * n, half // 3)] = dot_nt(hid[m], w_raw[rows, :])

        product(1 - core)
        copy = core_send(m, 0)
        product(core)
        yield
        copy.wait_recv()
        first = x_first(m, 1)
        yield
        second = x_second(m, 1, first)
        yield
        x_last(m, 1, second)
        columns = cols(fourth * zc, fourth)
        copy = send(remote(("z", m), xsum.at[m, 0, :, cols(fourth * (1 - zc), fourth)], zr.at[m, 0], zmate))
        yield
        copy.wait_recv()
        rows = cols(tq * x, tq)
        total = xsum[m, 0, :, columns] + zr[m, 0]
        total = total + gbuf[m, rows, cols(half * core + fourth * zc, fourth)]
        ob[m, core, rows, columns] = total
        gs[m] = total.astype(BF16)
        send(cross_copy(m))
        for copy in beyond_copies(m):
            send(copy)
        yield from spread(m)

    def cross_copy(m):
        return remote(("cross", m), shard_of(ob, m), bs.at[m], cross)

    def beyond_copies(m):
        return [
            remote(("beyond", i, m), gs.at[m], glow.at[m, b, core, cols(tq * x, tq), cols(fourth * zl, fourth)], to)
            for i, to in enumerate(beyond)
        ]

    @pl.when(s == 0)
    def _():
        interleave(down_chain, START_DOWN)


    def up_weights():
        for load in v_loads:
            load.wait()

        @pl.loop(0, tile // 128)
        def _(i):
            columns = cols(128 * i, 128)
            stripe[:tile, :] = v_raw[:, columns].astype(F32)
            for q in range(2):
                v_nat[q, :, columns] = stripe[pl.ds(q, half, stride=2), :].astype(BF16)

        w_load.wait()

        @pl.loop(0, half // 128)
        def _(i):
            for q in range(2):
                stripe[pl.ds(q, tile, stride=2), :] = w_raw[:, cols(half * q + 128 * i, 128)].astype(F32)
            w_nat[:, cols(128 * i, 128)] = stripe[...].astype(BF16)

    def up_chain(m):
        cross_copy(m).wait_recv()
        for copy in beyond_copies(m):
            copy.wait_recv()
        rows, columns = cols(tq * x, tq), cols(fourth * zc, fourth)
        glow[m, b, core, rows, columns] = bs[m].astype(BF16)
        for copies in ring_gather("g", m, lambda start, size: glow.at[m, :, core, cols(start, size)]):
            yield
        for copy in copies:
            copy.wait_recv()
        for part in range(2):
            columns = pl.ds(fourth * part, fourth)
            total = None
            for q in range(2):
                for k in range(2):
                    term = dot_nt(glow[m, q, k], v_nat[q, columns, k * half : (k + 1) * half])
                    total = term if total is None else total + term
            pf[m, :, columns] = total
            sb[m, :, columns] = total.astype(BF16)
        one = send(remote(("p1u", m), sb.at[m, pl.ds(0, th)], rl.at[m, 0], up))
        two = send(remote(("p1d", m), sb.at[m, pl.ds(th, th)], rl.at[m, 1], down))
        yield
        one.wait_recv()
        three = send(remote(("p2u", m), rl.at[m, 0], rp.at[m, pl.ds(0, th)], up))
        two.wait_recv()
        four = send(remote(("p2d", m), rl.at[m, 1], rp.at[m, pl.ds(th, th)], down))
        yield
        three.wait_recv()
        four.wait_recv()
        hid[m, :, :half] = ((pf[m] + rp[m].astype(F32)) * prev[m]).astype(BF16)

        def product(q, k):
            @pl.loop(0, 3)
            def _(n):
                rows = cols(tile * q + half * k + (half // 3) * n, half // 3)
                pb[m, q, k, :, cols((half // 3) * n, half // 3)] = dot_nt(hid[m, :, :half], w_nat[rows, :])

        copies = []
        for q in range(2):
            product(q, 1 - core)
            copies.append(core_send(m, q))
        for q in range(2):
            product(q, core)
        yield
        for copy in copies:
            copy.wait_recv()
        first = x_first(m, 2)
        yield
        second = x_second(m, 2, first)
        yield
        x_last(m, 2, second)
        copies = []
        for i, (to, q, zz) in enumerate(((corner, 1 - b, 1 - zc), (wmate, 1 - b, zc), (zmate, b, 1 - zc))):
            part = xsum.at[m, q, :, cols(fourth * zz, fourth)]
            copies.append(send(remote(("z", i, m), part, zr.at[m, i], to)))
        yield
        rows, columns = cols(tq * x, tq), cols(fourth * zc, fourth)
        total = xsum[m, b, :, columns]
        for i, copy in enumerate(copies):
            copy.wait_recv()
            total = total + zr[m, i]
        ob[m, core, rows, columns] = total + bs[m]
        yield from spread(m)

    @pl.when(s == 1)
    def _():
        up_weights()
        for m in range(chunks):
            pre_up[m].wait()
            slope_stage(m, half)
        interleave(up_chain, START_UP)


def local(grad_out, weight_in, weight_out, pre_act):
    batches, tok, tile = grad_out.shape
    chunks, whole, tok = batches * SPLIT, tok, tok // SPLIT
    half, fourth = tile // 2, tile // 4
    th, tq = tok // 2, tok // 4
    vmem = pltpu.VMEM
    scratch = [
        vmem((tile, tile), BF16),
        vmem((tile, tile), BF16),
        vmem((2, half, tile), BF16),
        vmem((2 * tile, half), BF16),
        vmem((2 * tile, 128), F32),
        vmem((chunks, tok, tile), F32),
        vmem((chunks, 2, 2, tok, half), BF16),
        vmem((chunks, tq, fourth), BF16),
        vmem((chunks, tok, half), F32),
        vmem((chunks, 4, tok, fourth), F32),
        vmem((chunks, 2, th, fourth), F32),
        vmem((chunks, 2, tok, fourth), F32),
        vmem((chunks, tok, tile), BF16),
        vmem((chunks, tok, half), F32),
        vmem((chunks, tok, half), BF16),
        vmem((chunks, 2, th, half), BF16),
        vmem((chunks, tok, half), BF16),
        vmem((chunks, 2, 2, tok, half), F32),
        vmem((chunks, 2, tok, half), F32),
        vmem((chunks, 3, 2, tq, half), BF16),
        vmem((chunks, 2, 2, tq // 2, half), BF16),
        vmem((chunks, 2, 2, tq, half), BF16),
        vmem((chunks, 2, tq, half), F32),
        vmem((chunks, 3, tq, fourth), F32),
        vmem((chunks, tq, fourth), F32),
        vmem((chunks, 2, tok, half), F32),
        pltpu.SemaphoreType.DMA((N_REMOTE,)),
        pltpu.SemaphoreType.DMA((N_REMOTE,)),
        pltpu.SemaphoreType.DMA((N_LOCAL,)),
    ]
    anywhere = pl.BlockSpec(memory_space=pl.ANY)
    return pl.pallas_call(
        kernel,
        out_shape=jax.ShapeDtypeStruct((1, batches, whole, tile), F32),
        in_specs=[anywhere] * 4,
        out_specs=anywhere,
        scratch_shapes=scratch,
        compiler_params=pltpu.CompilerParams(
            collective_id=0, has_side_effects=True, vmem_limit_bytes=67_000_000
        ),
    )(grad_out, weight_in, weight_out, pre_act)


def solution(mesh):
    return jax.shard_map(
        local,
        mesh=mesh,
        in_specs=(
            P(None, None, "wid"),
            P("section", "wid", "hid"),
            P("section", "hid", "wid"),
            P("section", None, None, "hid"),
        ),
        out_specs=P("section", None, None, "wid"),
        check_vma=False,
    )
```

time: 210 us -> 155 us (0.74)
  Pallas kernels: 204 us -> 151 us
    pallas_call x1, Pallas kernels: 204 us -> 151 us  [local(): pl.pallas_call(kernel, out_shape=jax.ShapeDtypeStruct((1, batches, whole,...]
where the time goes in v2:
time: 155 us
  Pallas kernels  151 us (97%)
  local copies, waits for them, and re-layouts  3.76 us (2%)
    pallas_call x1, Pallas kernels, local(): pl.pallas_call(kernel, out_shape=jax.ShapeDtypeStruct((1, batches, whole,...  151 us
    unnamed x1, local copies, waits for them, and re-layouts  3.76 us

profile of v2, /device:TPU:65, one launch (start us, length us, event | category | flops | bytes accessed | tf_op | source)
XLA Modules:
  0.0 154.6 jit_solution(1065569150677099091)
XLA Ops:
  0.0 150.8 %shard_map.46 = f32[1,2,256,1536]{3,2,1,0:T(8,128)} custom-call(f32[2,256,1536]{2,1,0:T(8,128)} %grad.1, bf16[1,1536,1536]{2,1,0:T(8,128)(2,1)} %win.1, bf16[1,1536,1536]{2,1,0:T(8,128)(2,1)} %wout.1, f32[1,2,256,1536]{3,2,1,0:T(8,128)} %pre.1), custom_call_target="tpu_custom_call" | custom-call | tf_op jit(solution)/shard_map/pallas_call | solution.py:471
  150.8 3.8 %copy.6 = f32[1,2,256,1536]{3,2,1,0:T(8,128)} copy(f32[1,2,256,1536]{3,2,1,0:T(8,128)} %shard_map.46) | data formatting | bytes 6291456

commit v3 on v2

--- a/solution.py
+++ b/solution.py
@@ -8,11 +8,11 @@
 F32 = jnp.float32
 BF16 = jnp.bfloat16
 MESH = pl.DeviceIdType.MESH
-N_REMOTE = 240
+N_REMOTE = 272
 N_LOCAL = 32
 SPLIT = 2
-START_DOWN = (0, 3, 5, 7)
-START_UP = (0, 2, 4, 6)
+START_DOWN = (0, 1, 2, 3)
+START_UP = (0, 1, 2, 3)
 NT = (((1,), (1,)), ((), ()))
 
 
@@ -22,14 +22,18 @@
     return normal_cdf + pre * density
 
 
+def dot_nn(a, b):
+    return lax.dot_general(a, b, (((1,), (0,)), ((), ())), preferred_element_type=F32)
+
+
 def dot_nt(a, b):
     return lax.dot_general(a, b, NT, preferred_element_type=F32)
 
 
 def kernel(
     grad, win, wout, pre, out,
-    v_raw, w_raw, v_nat, w_nat, stripe, gbuf, glow, gs, prev, pa, r1, r2, hid, pf, sb, rl, rp, pb, rc,
-    xs, xr1, xr2, xsum, zr, bs, ob,
+    v_raw, w_raw, vt, wt, stripe, gbuf, glow, gs, prev, pa, r1, r2, hid, pf, sb, rl, rp, pb, rc,
+    xs, xr1, xr2, xsum, zr, ds, bs, ob,
     send_sem, recv_sem, local_sem,
 ):
     s = lax.axis_index("section")
@@ -64,7 +68,7 @@
     corner = device(flip_w=True, flip_z=True)
     cross = device(flip_s=True, flip_z=True)
     beyond = [
-        device(flip_s=True), device(flip_s=True, flip_w=True), device(flip_s=True, flip_z=True, flip_w=True)
+        cross, device(flip_s=True), device(flip_s=True, flip_z=True, flip_w=True), device(flip_s=True, flip_w=True)
     ]
 
     keys = {}
@@ -133,10 +137,12 @@
             load.start()
 
     barrier = pltpu.get_barrier_semaphore()
-    peers = [right, left, up, down, mate, zmate, corner, cross, *beyond]
+    peers = [right, left, up, down, mate, zmate, corner, *beyond]
     for peer in peers:
         pl.semaphore_signal(barrier, inc=1, device_id=peer, device_id_type=MESH)
-    pl.semaphore_wait(barrier, len(peers))
+
+    def all_in():
+        pl.semaphore_wait(barrier, len(peers))
 
     def slope_stage(m, width):
         @pl.loop(0, 4)
@@ -258,6 +264,8 @@
             pa[m, r] = dot_nt(glow[m, 0, 0], v_raw[rows, :half]) + dot_nt(glow[m, 0, 1], v_raw[rows, half:])
 
         partial(2)
+        if m == 0:
+            all_in()
         one = send(remote(("a1u", m), pa.at[m, 2, pl.ds(0, th)], r1.at[m, 0], up))
         two = send(remote(("a1d", m), pa.at[m, 2, pl.ds(th, th)], r1.at[m, 1], down))
         partial(1)
@@ -295,10 +303,7 @@
             w_load.wait()
 
         def product(k):
-            @pl.loop(0, 3)
-            def _(n):
-                rows = cols(half * k + (half // 3) * n, half // 3)
-                pb[m, 0, k, :, cols((half // 3) * n, half // 3)] = dot_nt(hid[m], w_raw[rows, :])
+            pb[m, 0, k] = dot_nt(hid[m], w_raw[cols(half * k, half), :])
 
         product(1 - core)
         copy = core_send(m, 0)
@@ -316,16 +321,16 @@
         copy.wait_recv()
         rows = cols(tq * x, tq)
         total = xsum[m, 0, :, columns] + zr[m, 0]
-        total = total + gbuf[m, rows, cols(half * core + fourth * zc, fourth)]
-        ob[m, core, rows, columns] = total
-        gs[m] = total.astype(BF16)
-        send(cross_copy(m))
+        ds[m] = total
+        ob[m, core, rows, columns] = total.astype(BF16)
+        gs[m] = (total + gbuf[m, rows, cols(half * core + fourth * zc, fourth)]).astype(BF16)
         for copy in beyond_copies(m):
             send(copy)
+        send(cross_copy(m))
         yield from spread(m)
 
     def cross_copy(m):
-        return remote(("cross", m), shard_of(ob, m), bs.at[m], cross)
+        return remote(("cross", m), ds.at[m], bs.at[m], cross)
 
     def beyond_copies(m):
         return [
@@ -347,7 +352,7 @@
             columns = cols(128 * i, 128)
             stripe[:tile, :] = v_raw[:, columns].astype(F32)
             for q in range(2):
-                v_nat[q, :, columns] = stripe[pl.ds(q, half, stride=2), :].astype(BF16)
+                vt[q, columns, :] = stripe[pl.ds(q, half, stride=2), :].T.astype(BF16)
 
         w_load.wait()
 
@@ -355,44 +360,47 @@
         def _(i):
             for q in range(2):
                 stripe[pl.ds(q, tile, stride=2), :] = w_raw[:, cols(half * q + 128 * i, 128)].astype(F32)
-            w_nat[:, cols(128 * i, 128)] = stripe[...].astype(BF16)
+            wt[cols(128 * i, 128), :] = stripe[...].T.astype(BF16)
 
     def up_chain(m):
-        cross_copy(m).wait_recv()
         for copy in beyond_copies(m):
             copy.wait_recv()
-        rows, columns = cols(tq * x, tq), cols(fourth * zc, fourth)
-        glow[m, b, core, rows, columns] = bs[m].astype(BF16)
         for copies in ring_gather("g", m, lambda start, size: glow.at[m, :, core, cols(start, size)]):
             yield
         for copy in copies:
             copy.wait_recv()
+        swaps = []
         for part in range(2):
             columns = pl.ds(fourth * part, fourth)
             total = None
             for q in range(2):
                 for k in range(2):
-                    term = dot_nt(glow[m, q, k], v_nat[q, columns, k * half : (k + 1) * half])
+                    term = dot_nn(glow[m, q, k], vt[q, k * half : (k + 1) * half, columns])
                     total = term if total is None else total + term
             pf[m, :, columns] = total
-            sb[m, :, columns] = total.astype(BF16)
-        one = send(remote(("p1u", m), sb.at[m, pl.ds(0, th)], rl.at[m, 0], up))
-        two = send(remote(("p1d", m), sb.at[m, pl.ds(th, th)], rl.at[m, 1], down))
-        yield
-        one.wait_recv()
-        three = send(remote(("p2u", m), rl.at[m, 0], rp.at[m, pl.ds(0, th)], up))
-        two.wait_recv()
-        four = send(remote(("p2d", m), rl.at[m, 1], rp.at[m, pl.ds(th, th)], down))
-        yield
-        three.wait_recv()
-        four.wait_recv()
-        hid[m, :, :half] = ((pf[m] + rp[m].astype(F32)) * prev[m]).astype(BF16)
+            sb[m, part] = total.astype(BF16)
+            one = remote(("p1u", m, part), sb.at[m, part, pl.ds(0, th)], rl.at[m, part, 0], up)
+            two = remote(("p1d", m, part), sb.at[m, part, pl.ds(th, th)], rl.at[m, part, 1], down)
+            swaps.append((send(one), send(two)))
+        yield
+        relayed = []
+        for part, (one, two) in enumerate(swaps):
+            one.wait_recv()
+            three = remote(("p2u", m, part), rl.at[m, part, 0], rp.at[m, part, pl.ds(0, th)], up)
+            relayed.append(send(three))
+            two.wait_recv()
+            four = remote(("p2d", m, part), rl.at[m, part, 1], rp.at[m, part, pl.ds(th, th)], down)
+            relayed.append(send(four))
+        yield
+        for copy in relayed:
+            copy.wait_recv()
+        for part in range(2):
+            columns = pl.ds(fourth * part, fourth)
+            total = pf[m, :, columns] + rp[m, part].astype(F32)
+            hid[m, :, columns] = (total * prev[m, :, columns]).astype(BF16)
 
         def product(q, k):
-            @pl.loop(0, 3)
-            def _(n):
-                rows = cols(tile * q + half * k + (half // 3) * n, half // 3)
-                pb[m, q, k, :, cols((half // 3) * n, half // 3)] = dot_nt(hid[m, :, :half], w_nat[rows, :])
+            pb[m, q, k] = dot_nn(hid[m, :, :half], wt[:, cols(tile * q + half * k, half)])
 
         copies = []
         for q in range(2):
@@ -418,12 +426,14 @@
         for i, copy in enumerate(copies):
             copy.wait_recv()
             total = total + zr[m, i]
-        ob[m, core, rows, columns] = total + bs[m]
+        cross_copy(m).wait_recv()
+        ob[m, core, rows, columns] = (total + bs[m]).astype(BF16)
         yield from spread(m)
 
     @pl.when(s == 1)
     def _():
         up_weights()
+        all_in()
         for m in range(chunks):
             pre_up[m].wait()
             slope_stage(m, half)
@@ -439,8 +449,8 @@
     scratch = [
         vmem((tile, tile), BF16),
         vmem((tile, tile), BF16),
-        vmem((2, half, tile), BF16),
-        vmem((2 * tile, half), BF16),
+        vmem((2, tile, half), BF16),
+        vmem((half, 2 * tile), BF16),
         vmem((2 * tile, 128), F32),
         vmem((chunks, tok, tile), F32),
         vmem((chunks, 2, 2, tok, half), BF16),
@@ -451,9 +461,9 @@
         vmem((chunks, 2, tok, fourth), F32),
         vmem((chunks, tok, tile), BF16),
         vmem((chunks, tok, half), F32),
-        vmem((chunks, tok, half), BF16),
-        vmem((chunks, 2, th, half), BF16),
-        vmem((chunks, tok, half), BF16),
+        vmem((chunks, 2, tok, fourth), BF16),
+        vmem((chunks, 2, 2, th, fourth), BF16),
+        vmem((chunks, 2, tok, fourth), BF16),
         vmem((chunks, 2, 2, tok, half), F32),
         vmem((chunks, 2, tok, half), F32),
         vmem((chunks, 3, 2, tq, half), BF16),
@@ -462,15 +472,16 @@
         vmem((chunks, 2, tq, half), F32),
         vmem((chunks, 3, tq, fourth), F32),
         vmem((chunks, tq, fourth), F32),
-        vmem((chunks, 2, tok, half), F32),
+        vmem((chunks, tq, fourth), F32),
+        vmem((chunks, 2, tok, half), BF16),
         pltpu.SemaphoreType.DMA((N_REMOTE,)),
         pltpu.SemaphoreType.DMA((N_REMOTE,)),
         pltpu.SemaphoreType.DMA((N_LOCAL,)),
     ]
     anywhere = pl.BlockSpec(memory_space=pl.ANY)
-    return pl.pallas_call(
+    change = pl.pallas_call(
         kernel,
-        out_shape=jax.ShapeDtypeStruct((1, batches, whole, tile), F32),
+        out_shape=jax.ShapeDtypeStruct((1, batches, whole, tile), BF16),
         in_specs=[anywhere] * 4,
         out_specs=anywhere,
         scratch_shapes=scratch,
@@ -478,6 +489,7 @@
             collective_id=0, has_side_effects=True, vmem_limit_bytes=67_000_000
         ),
     )(grad_out, weight_in, weight_out, pre_act)
+    return grad_out[None] + change.astype(F32)
 
 
 def solution(mesh):

time: 155 us -> 131 us (0.85)
  Pallas kernels: 151 us -> 126 us
  other arithmetic: 0 us -> 4.52 us
  local copies, waits for them, and re-layouts: 3.76 us -> 0 us
    pallas_call x1, Pallas kernels: 151 us -> 126 us  [local(): pl.pallas_call(kernel, out_shape=jax.ShapeDtypeStruct((1, batches, whole,...]
    add x0 -> x1, other arithmetic: none -> 4.52 us  [local(): return grad_out[None] + change.astype(F32)]
    unnamed x1 -> x0, local copies, waits for them, and re-layouts: 3.76 us -> none
where the time goes in v3:
time: 131 us; the launch traced here: 130 us
  Pallas kernels  126 us (96%)
  other arithmetic  4.52 us (3%)
    pallas_call x1, Pallas kernels, local(): pl.pallas_call(kernel, out_shape=jax.ShapeDtypeStruct((1, batches, whole,...  126 us
    add x1, other arithmetic, local(): return grad_out[None] + change.astype(F32)  4.52 us

profile of v3, /device:TPU:65, one launch (start us, length us, event | category | flops | bytes accessed | tf_op | source)
XLA Modules:
  0.0 130.4 jit_solution(975339833581573380)
XLA Ops:
  0.0 125.9 %shard_map.46 = bf16[1,2,256,1536]{3,2,1,0:T(8,128)(2,1)} custom-call(f32[2,256,1536]{2,1,0:T(8,128)} %grad.1, bf16[1,1536,1536]{2,1,0:T(8,128)(2,1)} %win.1, bf16[1,1536,1536]{2,1,0:T(8,128)(2,1)} %wout.1, f32[1,2,256,1536]{3,2,1,0:T(8,128)} %pre.1), custom_call_target="tpu_custom_call" | custom-call | tf_op jit(solution)/shard_map/pallas_call | solution.py:482
  125.9 4.5 %bitcast_add_fusion = f32[1,2,256,1536]{3,2,1,0:T(8,128)} fusion(f32[2,256,1536]{2,1,0:T(8,128)} %grad.1, bf16[1,2,256,1536]{3,2,1,0:T(8,128)(2,1)} %shard_map.46), kind=kLoop, calls=%fused_computation | loop fusion | flops 1572864 | bytes 7864320 | tf_op jit(solution)/shard_map/add | solution.py:492

commit v4 on v3

--- a/solution.py
+++ b/solution.py
@@ -1,3 +1,5 @@
+import functools
+
 import jax
 import jax.numpy as jnp
 from jax import lax
@@ -22,6 +24,24 @@
     return normal_cdf + pre * density
 
 
+def pack(ref, value):
+    rows, columns = value.shape
+    blocks = [value[:, i : i + 128] for i in range(0, columns, 128)]
+    top = functools.reduce(jnp.maximum, [jnp.max(jnp.abs(block), axis=0, keepdims=True) for block in blocks])
+    scale = (80.0 / jnp.maximum(top, 1e-30)).astype(BF16)
+    for i, block in enumerate(blocks):
+        ref[rows * i : rows * (i + 1), :] = jnp.exp(block * scale.astype(F32)).astype(BF16)
+    ref[rows * len(blocks) :, :] = jnp.broadcast_to(scale.astype(F32), (16, 128)).astype(BF16)
+
+
+def unpack(ref, rows, columns):
+    count = columns // 128
+    step = 1.0 / ref[rows * count :, :].astype(F32)[:1]
+    return jnp.concatenate(
+        [jnp.log(ref[rows * i : rows * (i + 1), :].astype(F32)) * step for i in range(count)], axis=1
+    )
+
+
 def dot_nn(a, b):
     return lax.dot_general(a, b, (((1,), (0,)), ((), ())), preferred_element_type=F32)
 
@@ -32,8 +52,8 @@
 
 def kernel(
     grad, win, wout, pre, out,
-    v_raw, w_raw, vt, wt, stripe, gbuf, glow, gs, prev, pa, r1, r2, hid, pf, sb, rl, rp, pb, rc,
-    xs, xr1, xr2, xsum, zr, ds, bs, ob,
+    v_raw, w_raw, vt, wt, stripe, gbuf, gd, glow, gs, prev, pa, a1, a2, r1, r2, hid, pf, sb, rl, rp, pb, rc,
+    xs, xr1, xr2, xsum, zs, zr, ds, bs, ob,
     send_sem, recv_sem, local_sem,
 ):
     s = lax.axis_index("section")
@@ -44,7 +64,6 @@
     core = lax.rem(h, 2)
     c = lax.div(w, 2)
     b = lax.rem(w, 2)
-    zc = zl + s - 2 * zl * s
     tile = grad.shape[2]
     chunks, tok = pb.shape[0], pb.shape[3]
     half, fourth = tile // 2, tile // 4
@@ -67,9 +86,7 @@
     wmate = device(flip_w=True)
     corner = device(flip_w=True, flip_z=True)
     cross = device(flip_s=True, flip_z=True)
-    beyond = [
-        cross, device(flip_s=True), device(flip_s=True, flip_z=True, flip_w=True), device(flip_s=True, flip_w=True)
-    ]
+    beyond = [cross, device(flip_s=True, flip_z=True, flip_w=True)]
 
     keys = {}
 
@@ -116,7 +133,7 @@
         for r in (2, 1, 3, 0)
     ]
     w_load = local("w", win.at[0], w_raw)
-    g_loads = [local(("g", m), grad.at[span(m)], gbuf.at[m]) for m in range(chunks)]
+    g_loads = [local(("g", m), grad.at[m], gbuf.at[m]) for m in range(chunks // SPLIT)]
 
     @pl.when(s == 0)
     def _():
@@ -193,9 +210,6 @@
 
     last = []
 
-    def shard_of(ref, m):
-        return ref.at[m, core, cols(tq * x, tq), cols(fourth * zc, fourth)]
-
     def ring_gather(name, m, block):
         own = block(tq * x, tq)
         to_right = send(remote((name, "1r", m), own, own, right))
@@ -219,9 +233,6 @@
         yield copies
 
     def spread(m):
-        first = send(remote(("oz", m), shard_of(ob, m), shard_of(ob, m), zmate))
-        yield
-        first.wait_recv()
         for copies in ring_gather("o", m, lambda start, size: ob.at[m, core, cols(start, size)]):
             if copies is None:
                 yield
@@ -253,38 +264,47 @@
 
 
     def down_chain(m):
-        g_loads[m].wait()
-        for k in range(2):
-            glow[m, 0, k] = gbuf[m, :, k * half : (k + 1) * half].astype(BF16)
+        batch, rows = m // SPLIT, pl.ds(tok * (m % SPLIT), tok)
 
         def partial(r):
             if m == 0:
                 v_loads[(2, 1, 3, 0).index(r)].wait()
-            rows = cols(fourth * of4(w + r), fourth)
-            pa[m, r] = dot_nt(glow[m, 0, 0], v_raw[rows, :half]) + dot_nt(glow[m, 0, 1], v_raw[rows, half:])
-
-        partial(2)
+            units = cols(fourth * of4(w + r), fourth)
+            pa[batch, r] = dot_nt(gd[batch, 0], v_raw[units, :half]) + dot_nt(gd[batch, 1], v_raw[units, half:])
+
+        if m % SPLIT == 0:
+            g_loads[batch].wait()
+            for k in range(2):
+                gd[batch, k] = gbuf[batch, :, k * half : (k + 1) * half].astype(BF16)
+            partial(2)
         if m == 0:
             all_in()
-        one = send(remote(("a1u", m), pa.at[m, 2, pl.ds(0, th)], r1.at[m, 0], up))
-        two = send(remote(("a1d", m), pa.at[m, 2, pl.ds(th, th)], r1.at[m, 1], down))
-        partial(1)
-        partial(3)
+        first = pa[batch, 2, rows]
+        pack(a1.at[m, 0], first[:th])
+        one = send(remote(("a1u", m), a1.at[m, 0], r1.at[m, 0], up))
+        pack(a1.at[m, 1], first[th:])
+        two = send(remote(("a1d", m), a1.at[m, 1], r1.at[m, 1], down))
+        if m % SPLIT == 0:
+            partial(1)
+            partial(3)
         yield
         one.wait_recv()
-        pa[m, 1, :th] += r1[m, 0]
-        three = send(remote(("a2u", m), pa.at[m, 1], r2.at[m, 0], up))
+        part = pa[batch, 1, rows]
+        pack(a2.at[m, 0], jnp.concatenate([part[:th] + unpack(r1.at[m, 0], th, fourth), part[th:]], axis=0))
+        three = send(remote(("a2u", m), a2.at[m, 0], r2.at[m, 0], up))
         two.wait_recv()
-        pa[m, 3, th:] += r1[m, 1]
-        four = send(remote(("a2d", m), pa.at[m, 3], r2.at[m, 1], down))
-        partial(0)
+        part = pa[batch, 3, rows]
+        pack(a2.at[m, 1], jnp.concatenate([part[:th], part[th:] + unpack(r1.at[m, 1], th, fourth)], axis=0))
+        four = send(remote(("a2d", m), a2.at[m, 1], r2.at[m, 1], down))
+        if m % SPLIT == 0:
+            partial(0)
         pre_down[m].wait()
         slope_stage(m, fourth)
         yield
         three.wait_recv()
         four.wait_recv()
         mine = cols(fourth * w, fourth)
-        total = pa[m, 0] + r2[m, 0] + r2[m, 1]
+        total = pa[batch, 0, rows] + unpack(r2.at[m, 0], tok, fourth) + unpack(r2.at[m, 1], tok, fourth)
         hid[m, :, mine] = (total * prev[m, :, :fourth]).astype(BF16)
         own = hid.at[m, :, mine]
         to_up = send(remote(("h1u", m), own, own, up))
@@ -315,18 +335,19 @@
         second = x_second(m, 1, first)
         yield
         x_last(m, 1, second)
-        columns = cols(fourth * zc, fourth)
-        copy = send(remote(("z", m), xsum.at[m, 0, :, cols(fourth * (1 - zc), fourth)], zr.at[m, 0], zmate))
+        pack(zs.at[m, 0], xsum[m, 0])
+        copy = send(remote(("z", 0, m), zs.at[m, 0], zr.at[m, 0], zmate))
         yield
         copy.wait_recv()
         rows = cols(tq * x, tq)
-        total = xsum[m, 0, :, columns] + zr[m, 0]
-        ds[m] = total
-        ob[m, core, rows, columns] = total.astype(BF16)
-        gs[m] = (total + gbuf[m, rows, cols(half * core + fourth * zc, fourth)]).astype(BF16)
+        total = unpack(zs.at[m, 0], tq, half) + unpack(zr.at[m, 0], tq, half)
+        grad_rows = pl.ds(pl.multiple_of(tok * (m % SPLIT) + tq * x, tq), tq)
+        gs[m] = (total + gbuf[m // SPLIT, grad_rows, cols(half * core, half)]).astype(BF16)
         for copy in beyond_copies(m):
             send(copy)
+        pack(ds.at[m], total)
         send(cross_copy(m))
+        ob[m, core, rows] = total.astype(BF16)
         yield from spread(m)
 
     def cross_copy(m):
@@ -334,7 +355,7 @@
 
     def beyond_copies(m):
         return [
-            remote(("beyond", i, m), gs.at[m], glow.at[m, b, core, cols(tq * x, tq), cols(fourth * zl, fourth)], to)
+            remote(("beyond", i, m), gs.at[m], glow.at[m, b, core, cols(tq * x, tq)], to)
             for i, to in enumerate(beyond)
         ]
 
@@ -416,18 +437,17 @@
         second = x_second(m, 2, first)
         yield
         x_last(m, 2, second)
-        copies = []
-        for i, (to, q, zz) in enumerate(((corner, 1 - b, 1 - zc), (wmate, 1 - b, zc), (zmate, b, 1 - zc))):
-            part = xsum.at[m, q, :, cols(fourth * zz, fourth)]
-            copies.append(send(remote(("z", i, m), part, zr.at[m, i], to)))
-        yield
-        rows, columns = cols(tq * x, tq), cols(fourth * zc, fourth)
-        total = xsum[m, b, :, columns]
-        for i, copy in enumerate(copies):
-            copy.wait_recv()
-            total = total + zr[m, i]
+        pack(zs.at[m, 1], xsum[m, 1 - b])
+        copies = [send(remote(("z", i, m), zs.at[m, 1], zr.at[m, i], to)) for i, to in ((2, corner), (1, wmate))]
+        pack(zs.at[m, 0], xsum[m, b])
+        copies.append(send(remote(("z", 0, m), zs.at[m, 0], zr.at[m, 0], zmate)))
+        yield
+        for copy in copies:
+            copy.wait_recv()
         cross_copy(m).wait_recv()
-        ob[m, core, rows, columns] = (total + bs[m]).astype(BF16)
+        terms = [unpack(part, tq, half) for part in (zs.at[m, 0], zr.at[m, 0], zr.at[m, 1], zr.at[m, 2])]
+        total = (terms[0] + terms[1]) + (terms[2] + terms[3])
+        ob[m, core, cols(tq * x, tq)] = (total + unpack(bs.at[m], tq, half)).astype(BF16)
         yield from spread(m)
 
     @pl.when(s == 1)
@@ -452,13 +472,16 @@
         vmem((2, tile, half), BF16),
         vmem((half, 2 * tile), BF16),
         vmem((2 * tile, 128), F32),
-        vmem((chunks, tok, tile), F32),
+        vmem((batches, whole, tile), F32),
+        vmem((batches, 2, whole, half), BF16),
         vmem((chunks, 2, 2, tok, half), BF16),
-        vmem((chunks, tq, fourth), BF16),
+        vmem((chunks, tq, half), BF16),
         vmem((chunks, tok, half), F32),
-        vmem((chunks, 4, tok, fourth), F32),
-        vmem((chunks, 2, th, fourth), F32),
-        vmem((chunks, 2, tok, fourth), F32),
+        vmem((batches, 4, whole, fourth), F32),
+        vmem((chunks, 2, th * fourth // 128 + 16, 128), BF16),
+        vmem((chunks, 2, tok * fourth // 128 + 16, 128), BF16),
+        vmem((chunks, 2, th * fourth // 128 + 16, 128), BF16),
+        vmem((chunks, 2, tok * fourth // 128 + 16, 128), BF16),
         vmem((chunks, tok, tile), BF16),
         vmem((chunks, tok, half), F32),
         vmem((chunks, 2, tok, fourth), BF16),
@@ -470,9 +493,10 @@
         vmem((chunks, 2, 2, tq // 2, half), BF16),
         vmem((chunks, 2, 2, tq, half), BF16),
         vmem((chunks, 2, tq, half), F32),
-        vmem((chunks, 3, tq, fourth), F32),
-        vmem((chunks, tq, fourth), F32),
-        vmem((chunks, tq, fourth), F32),
+        vmem((chunks, 2, tq * half // 128 + 16, 128), BF16),
+        vmem((chunks, 3, tq * half // 128 + 16, 128), BF16),
+        vmem((chunks, tq * half // 128 + 16, 128), BF16),
+        vmem((chunks, tq * half // 128 + 16, 128), BF16),
         vmem((chunks, 2, tok, half), BF16),
         pltpu.SemaphoreType.DMA((N_REMOTE,)),
         pltpu.SemaphoreType.DMA((N_REMOTE,)),
@@ -486,7 +510,7 @@
         out_specs=anywhere,
         scratch_shapes=scratch,
         compiler_params=pltpu.CompilerParams(
-            collective_id=0, has_side_effects=True, vmem_limit_bytes=67_000_000
+            collective_id=0, has_side_effects=True, vmem_limit_bytes=60_000_000
         ),
     )(grad_out, weight_in, weight_out, pre_act)
     return grad_out[None] + change.astype(F32)

time: 131 us -> 118 us (0.901)
  Pallas kernels: 126 us -> 114 us
    pallas_call x1, Pallas kernels: 126 us -> 114 us  [local(): pl.pallas_call(kernel, out_shape=jax.ShapeDtypeStruct((1, batches, whole,...]
where the time goes in v4:
time: 118 us
  Pallas kernels  114 us (97%)
  other arithmetic  3.58 us (3%)
    pallas_call x1, Pallas kernels, local(): pl.pallas_call(kernel, out_shape=jax.ShapeDtypeStruct((1, batches, whole,...  114 us
    add x1, other arithmetic, local(): return grad_out[None] + change.astype(F32)  3.58 us

profile of v4, /device:TPU:65, one launch (start us, length us, event | category | flops | bytes accessed | tf_op | source)
XLA Modules:
  0.0 117.9 jit_solution(2163333355547212324)
XLA Ops:
  0.0 0.0 copy-start
  0.0 114.3 %shard_map.46 = bf16[1,2,256,1536]{3,2,1,0:T(8,128)(2,1)} custom-call(f32[2,256,1536]{2,1,0:T(8,128)} %grad.1, bf16[1,1536,1536]{2,1,0:T(8,128)(2,1)} %win.1, bf16[1,1536,1536]{2,1,0:T(8,128)(2,1)} %wout.1, f32[1,2,256,1536]{3,2,1,0:T(8,128)} %pre.1), custom_call_target="tpu_custom_call" | custom-call | tf_op jit(solution)/shard_map/pallas_call | solution.py:506
  114.3 0.0 copy-done
  114.3 3.6 %bitcast_add_fusion = f32[1,2,256,1536]{3,2,1,0:T(8,128)} fusion(f32[2,256,1536]{2,1,0:T(8,128)S(1)} %copy-done, bf16[1,2,256,1536]{3,2,1,0:T(8,128)(2,1)} %shard_map.46), kind=kLoop, calls=%fused_computation | loop fusion | flops 1572864 | bytes 7864320 | tf_op jit(solution)/shard_map/add | solution.py:516
Async XLA Ops:
  0.0 114.3 %copy-start = (f32[2,256,1536]{2,1,0:T(8,128)S(1)}, f32[2,256,1536]{2,1,0:T(8,128)}, u32[]{:S(2)}) copy-start(f32[2,256,1536]{2,1,0:T(8,128)} %grad.1) | copy-start | bytes 9437188

commit v5 on v4

--- a/solution.py
+++ b/solution.py
@@ -12,9 +12,10 @@
 MESH = pl.DeviceIdType.MESH
 N_REMOTE = 272
 N_LOCAL = 32
+PIECES = 6
 SPLIT = 2
 START_DOWN = (0, 1, 2, 3)
-START_UP = (0, 1, 2, 3)
+START_UP = (0, 1, 2, 2)
 NT = (((1,), (1,)), ((), ()))
 
 
@@ -53,7 +54,7 @@
 def kernel(
     grad, win, wout, pre, out,
     v_raw, w_raw, vt, wt, stripe, gbuf, gd, glow, gs, prev, pa, a1, a2, r1, r2, hid, pf, sb, rl, rp, pb, rc,
-    xs, xr1, xr2, xsum, zs, zr, ds, bs, ob,
+    xs1, xs2, xr1, xr2, xsum, zs, zr, ds, bs,
     send_sem, recv_sem, local_sem,
 ):
     s = lax.axis_index("section")
@@ -178,37 +179,39 @@
         rows = x_rows(r)
         return pb[m, q, core, rows, :] + rc[m, q, rows, :]
 
+    def x_block(m, nq, r):
+        return jnp.concatenate([chip_sum(m, q, r) for q in range(nq)], axis=1)
+
     def x_first(m, nq):
-        for q in range(nq):
-            xs[m, 0, q] = chip_sum(m, q, 2).astype(BF16)
-        one = remote(("x1r", m), xs.at[m, 0, pl.ds(0, nq), pl.ds(0, te)], xr1.at[m, 0, pl.ds(0, nq)], right)
-        two = remote(("x1l", m), xs.at[m, 0, pl.ds(0, nq), pl.ds(te, te)], xr1.at[m, 1, pl.ds(0, nq)], left)
-        return send(one), send(two)
+        total = x_block(m, nq, 2)
+        used = pl.ds(0, te * nq * half // 128 + 16)
+        copies = []
+        for side, (name, to) in enumerate((("x1r", right), ("x1l", left))):
+            pack(xs1.at[m, side, used], total[te * side : te * (side + 1)])
+            copies.append(send(remote((name, m), xs1.at[m, side, used], xr1.at[m, side, used], to)))
+        return copies
 
     def x_second(m, nq, first):
         result = []
         for side, (copy, r, to) in enumerate(((first[0], 1, right), (first[1], 3, left))):
             copy.wait_recv()
-            lo = te * side
-            for q in range(nq):
-                total = chip_sum(m, q, r)
-                xs[m, 1 + side, q] = total.astype(BF16)
-                part = total[lo : lo + te] + xr1[m, side, q].astype(F32)
-                xs[m, 1 + side, q, lo : lo + te] = part.astype(BF16)
-            copy = remote(
-                ("x2", m, side), xs.at[m, 1 + side, pl.ds(0, nq)], xr2.at[m, side, pl.ds(0, nq)], to
-            )
-            result.append(send(copy))
+            total = x_block(m, nq, r)
+            came = unpack(xr1.at[m, side, pl.ds(0, te * nq * half // 128 + 16)], te, nq * half)
+            parts = [total[:te], total[te:]]
+            parts[side] = parts[side] + came
+            used = pl.ds(0, tq * nq * half // 128 + 16)
+            pack(xs2.at[m, side, used], jnp.concatenate(parts, axis=0))
+            result.append(send(remote(("x2", m, side), xs2.at[m, side, used], xr2.at[m, side, used], to)))
         return result
 
     def x_last(m, nq, second):
-        for copy in second:
-            copy.wait_recv()
+        total = x_block(m, nq, 0)
+        for side, copy in enumerate(second):
+            copy.wait_recv()
+            total = total + unpack(xr2.at[m, side, pl.ds(0, tq * nq * half // 128 + 16)], tq, nq * half)
         for q in range(nq):
-            xsum[m, q] = chip_sum(m, q, 0) + xr2[m, 0, q].astype(F32) + xr2[m, 1, q].astype(F32)
-
-
-    last = []
+            xsum[m, q] = total[:, half * q : half * (q + 1)]
+
 
     def ring_gather(name, m, block):
         own = block(tq * x, tq)
@@ -233,18 +236,14 @@
         yield copies
 
     def spread(m):
-        for copies in ring_gather("o", m, lambda start, size: ob.at[m, core, cols(start, size)]):
-            if copies is None:
-                yield
-        mine = local(("om", m), ob.at[m, core], out.at[(0, *span(m), cols(half * core, half))])
-        mine.start()
-        last.append(mine)
-        yield
+        for copies in ring_gather("o", m, lambda start, size: out.at[out_block(m, start, size)]):
+            yield
         for copy in copies:
             copy.wait_recv()
-        other = local(("oo", m), ob.at[m, 1 - core], out.at[(0, *span(m), cols(half * (1 - core), half))])
-        other.start()
-        last.append(other)
+
+    def out_block(m, start, size):
+        first = tok * (m % SPLIT)
+        return 0, m // SPLIT, pl.ds(pl.multiple_of(first + start, size), size), cols(half * core, half)
 
     def interleave(chain, start):
         steps = [chain(m) for m in range(chunks)]
@@ -255,13 +254,20 @@
                 if turn >= start[m] and next(steps[m], alive) is alive:
                     alive.discard(m)
             turn += 1
-        for copy in last:
-            copy.wait()
         for copy in started:
             copy.wait_send()
-        last.clear()
         started.clear()
 
+
+    def turn_weights(piece):
+        if piece == 0:
+            w_load.wait()
+
+        @pl.loop(0, tile // 128 // PIECES)
+        def _(i):
+            columns = cols(128 * (tile // 128 // PIECES * piece + i), 128)
+            for k in range(2):
+                vt[k, columns, :] = w_raw[k * half : (k + 1) * half, columns].astype(F32).T.astype(BF16)
 
     def down_chain(m):
         batch, rows = m // SPLIT, pl.ds(tok * (m % SPLIT), tok)
@@ -287,6 +293,8 @@
         if m % SPLIT == 0:
             partial(1)
             partial(3)
+        for piece in {0: (0, 1), 1: (2, 3), 2: (5,)}.get(m, ()):
+            turn_weights(piece)
         yield
         one.wait_recv()
         part = pa[batch, 1, rows]
@@ -300,6 +308,8 @@
             partial(0)
         pre_down[m].wait()
         slope_stage(m, fourth)
+        if m == 1:
+            turn_weights(4)
         yield
         three.wait_recv()
         four.wait_recv()
@@ -319,11 +329,9 @@
         yield
         on_up.wait_recv()
         on_down.wait_recv()
-        if m == 0:
-            w_load.wait()
 
         def product(k):
-            pb[m, 0, k] = dot_nt(hid[m], w_raw[cols(half * k, half), :])
+            pb[m, 0, k] = dot_nn(hid[m], vt[k])
 
         product(1 - core)
         copy = core_send(m, 0)
@@ -347,7 +355,7 @@
             send(copy)
         pack(ds.at[m], total)
         send(cross_copy(m))
-        ob[m, core, rows] = total.astype(BF16)
+        out[out_block(m, tq * x, tq)] = total.astype(BF16)
         yield from spread(m)
 
     def cross_copy(m):
@@ -399,25 +407,27 @@
                     term = dot_nn(glow[m, q, k], vt[q, k * half : (k + 1) * half, columns])
                     total = term if total is None else total + term
             pf[m, :, columns] = total
-            sb[m, part] = total.astype(BF16)
-            one = remote(("p1u", m, part), sb.at[m, part, pl.ds(0, th)], rl.at[m, part, 0], up)
-            two = remote(("p1d", m, part), sb.at[m, part, pl.ds(th, th)], rl.at[m, part, 1], down)
-            swaps.append((send(one), send(two)))
+            pack(sb.at[m, part, 0], total[:th])
+            one = send(remote(("p1u", m, part), sb.at[m, part, 0], rl.at[m, part, 0], up))
+            pack(sb.at[m, part, 1], total[th:])
+            two = send(remote(("p1d", m, part), sb.at[m, part, 1], rl.at[m, part, 1], down))
+            swaps.append((one, two))
         yield
         relayed = []
         for part, (one, two) in enumerate(swaps):
             one.wait_recv()
-            three = remote(("p2u", m, part), rl.at[m, part, 0], rp.at[m, part, pl.ds(0, th)], up)
+            three = remote(("p2u", m, part), rl.at[m, part, 0], rp.at[m, part, 0], up)
             relayed.append(send(three))
             two.wait_recv()
-            four = remote(("p2d", m, part), rl.at[m, part, 1], rp.at[m, part, pl.ds(th, th)], down)
+            four = remote(("p2d", m, part), rl.at[m, part, 1], rp.at[m, part, 1], down)
             relayed.append(send(four))
         yield
         for copy in relayed:
             copy.wait_recv()
         for part in range(2):
             columns = pl.ds(fourth * part, fourth)
-            total = pf[m, :, columns] + rp[m, part].astype(F32)
+            came = [unpack(rp.at[m, part, i], th, fourth) for i in range(2)]
+            total = pf[m, :, columns] + jnp.concatenate(came, axis=0)
             hid[m, :, columns] = (total * prev[m, :, columns]).astype(BF16)
 
         def product(q, k):
@@ -447,7 +457,7 @@
         cross_copy(m).wait_recv()
         terms = [unpack(part, tq, half) for part in (zs.at[m, 0], zr.at[m, 0], zr.at[m, 1], zr.at[m, 2])]
         total = (terms[0] + terms[1]) + (terms[2] + terms[3])
-        ob[m, core, cols(tq * x, tq)] = (total + unpack(bs.at[m], tq, half)).astype(BF16)
+        out[out_block(m, tq * x, tq)] = (total + unpack(bs.at[m], tq, half)).astype(BF16)
         yield from spread(m)
 
     @pl.when(s == 1)
@@ -484,20 +494,20 @@
         vmem((chunks, 2, tok * fourth // 128 + 16, 128), BF16),
         vmem((chunks, tok, tile), BF16),
         vmem((chunks, tok, half), F32),
-        vmem((chunks, 2, tok, fourth), BF16),
-        vmem((chunks, 2, 2, th, fourth), BF16),
-        vmem((chunks, 2, tok, fourth), BF16),
+        vmem((chunks, 2, 2, th * fourth // 128 + 16, 128), BF16),
+        vmem((chunks, 2, 2, th * fourth // 128 + 16, 128), BF16),
+        vmem((chunks, 2, 2, th * fourth // 128 + 16, 128), BF16),
         vmem((chunks, 2, 2, tok, half), F32),
         vmem((chunks, 2, tok, half), F32),
-        vmem((chunks, 3, 2, tq, half), BF16),
-        vmem((chunks, 2, 2, tq // 2, half), BF16),
-        vmem((chunks, 2, 2, tq, half), BF16),
+        vmem((chunks, 2, tq * half // 128 + 16, 128), BF16),
+        vmem((chunks, 2, tq * tile // 128 + 16, 128), BF16),
+        vmem((chunks, 2, tq * half // 128 + 16, 128), BF16),
+        vmem((chunks, 2, tq * tile // 128 + 16, 128), BF16),
         vmem((chunks, 2, tq, half), F32),
         vmem((chunks, 2, tq * half // 128 + 16, 128), BF16),
         vmem((chunks, 3, tq * half // 128 + 16, 128), BF16),
         vmem((chunks, tq * half // 128 + 16, 128), BF16),
         vmem((chunks, tq * half // 128 + 16, 128), BF16),
-        vmem((chunks, 2, tok, half), BF16),
         pltpu.SemaphoreType.DMA((N_REMOTE,)),
         pltpu.SemaphoreType.DMA((N_REMOTE,)),
         pltpu.SemaphoreType.DMA((N_LOCAL,)),
@@ -505,9 +515,9 @@
     anywhere = pl.BlockSpec(memory_space=pl.ANY)
     change = pl.pallas_call(
         kernel,
-        out_shape=jax.ShapeDtypeStruct((1, batches, whole, tile), BF16),
+        out_shape=vmem((1, batches, whole, tile), BF16),
         in_specs=[anywhere] * 4,
-        out_specs=anywhere,
+        out_specs=pl.BlockSpec(memory_space=vmem),
         scratch_shapes=scratch,
         compiler_params=pltpu.CompilerParams(
             collective_id=0, has_side_effects=True, vmem_limit_bytes=60_000_000

time: 118 us -> 115 us (0.975)
  other arithmetic: 3.58 us -> 2.12 us
    pallas_call x1, Pallas kernels: 114 us -> 113 us  [local(): pl.pallas_call(kernel, out_shape=vmem((1, batches, whole, tile), BF16), i...]
    add x1, other arithmetic: 3.58 us -> 2.12 us  [local(): return grad_out[None] + change.astype(F32)]
where the time goes in v5:
time: 115 us
  Pallas kernels  113 us (98%)
  other arithmetic  2.12 us (2%)
    pallas_call x1, Pallas kernels, local(): pl.pallas_call(kernel, out_shape=vmem((1, batches, whole, tile), BF16), i...  113 us

profile of v5, /device:TPU:65, one launch (start us, length us, event | category | flops | bytes accessed | tf_op | source)
XLA Modules:
  0.0 114.9 jit_solution(9595792833588822738)
XLA Ops:
  0.0 0.0 copy-start
  0.0 112.8 %shard_map.46 = bf16[1,2,256,1536]{3,2,1,0:T(8,128)(2,1)S(1)} custom-call(f32[2,256,1536]{2,1,0:T(8,128)} %grad.1, bf16[1,1536,1536]{2,1,0:T(8,128)(2,1)} %win.1, bf16[1,1536,1536]{2,1,0:T(8,128)(2,1)} %wout.1, f32[1,2,256,1536]{3,2,1,0:T(8,128)} %pre.1), custom_call_target="tpu_custom_call" | custom-call | tf_op jit(solution)/shard_map/pallas_call | solution.py:516
  112.8 0.0 copy-done
  112.8 2.1 %bitcast_add_fusion = f32[1,2,256,1536]{3,2,1,0:T(8,128)} fusion(f32[2,256,1536]{2,1,0:T(8,128)S(1)} %copy-done, bf16[1,2,256,1536]{3,2,1,0:T(8,128)(2,1)S(1)} %shard_map.46), kind=kLoop, calls=%fused_computation | loop fusion | flops 1572864 | bytes 7864320 | tf_op jit(solution)/shard_map/add | solution.py:526
Async XLA Ops:
  0.0 112.8 %copy-start = (f32[2,256,1536]{2,1,0:T(8,128)S(1)}, f32[2,256,1536]{2,1,0:T(8,128)}, u32[]{:S(2)}) copy-start(f32[2,256,1536]{2,1,0:T(8,128)} %grad.1) | copy-start | bytes 9437188

commit v6 on v5

--- a/solution.py
+++ b/solution.py
@@ -13,6 +13,10 @@
 N_REMOTE = 272
 N_LOCAL = 32
 PIECES = 6
+DIRECT = True
+DIRECT_OUT = True
+HOLD = 1
+FAST = (0,)
 SPLIT = 2
 START_DOWN = (0, 1, 2, 3)
 START_UP = (0, 1, 2, 2)
@@ -54,7 +58,7 @@
 def kernel(
     grad, win, wout, pre, out,
     v_raw, w_raw, vt, wt, stripe, gbuf, gd, glow, gs, prev, pa, a1, a2, r1, r2, hid, pf, sb, rl, rp, pb, rc,
-    xs1, xs2, xr1, xr2, xsum, zs, zr, ds, bs,
+    xs1, xs2, xr1, xr2, xr3, xsum, zs, zr, ds, bs,
     send_sem, recv_sem, local_sem,
 ):
     s = lax.axis_index("section")
@@ -86,6 +90,8 @@
     zmate = device(flip_z=True)
     wmate = device(flip_w=True)
     corner = device(flip_w=True, flip_z=True)
+    right_z, left_z = device(dx=1, flip_z=True), device(dx=-1, flip_z=True)
+    right_mate, left_mate = device(dx=1, flip_core=True), device(dx=-1, flip_core=True)
     cross = device(flip_s=True, flip_z=True)
     beyond = [cross, device(flip_s=True, flip_z=True, flip_w=True)]
 
@@ -155,7 +161,7 @@
             load.start()
 
     barrier = pltpu.get_barrier_semaphore()
-    peers = [right, left, up, down, mate, zmate, corner, *beyond]
+    peers = [right, left, up, down, mate, zmate, corner, right_z, left_z, right_mate, left_mate, *beyond]
     for peer in peers:
         pl.semaphore_signal(barrier, inc=1, device_id=peer, device_id_type=MESH)
 
@@ -191,7 +197,7 @@
             copies.append(send(remote((name, m), xs1.at[m, side, used], xr1.at[m, side, used], to)))
         return copies
 
-    def x_second(m, nq, first):
+    def x_second(m, nq, first, twins=()):
         result = []
         for side, (copy, r, to) in enumerate(((first[0], 1, right), (first[1], 3, left))):
             copy.wait_recv()
@@ -202,6 +208,9 @@
             used = pl.ds(0, tq * nq * half // 128 + 16)
             pack(xs2.at[m, side, used], jnp.concatenate(parts, axis=0))
             result.append(send(remote(("x2", m, side), xs2.at[m, side, used], xr2.at[m, side, used], to)))
+        for side, to in enumerate(twins):
+            used = pl.ds(0, tq * nq * half // 128 + 16)
+            result.append(send(remote(("x3", m, side), xs2.at[m, side, used], xr3.at[m, side], to)))
         return result
 
     def x_last(m, nq, second):
@@ -213,7 +222,7 @@
             xsum[m, q] = total[:, half * q : half * (q + 1)]
 
 
-    def ring_gather(name, m, block):
+    def ring_gather(name, m, block, direct):
         own = block(tq * x, tq)
         to_right = send(remote((name, "1r", m), own, own, right))
         to_left = send(remote((name, "1l", m), own, own, left))
@@ -228,16 +237,22 @@
         for i in (1, 3):
             piece = block(tq * of4(x + i), tq)
             copies.append(send(remote((name, "c", i, m), piece, piece, mate)))
+        if direct:
+            piece = block(tq * of4(x - 1), te)
+            copies.append(send(remote((name, "3r", m), piece, piece, right_mate)))
+            piece = block(tq * of4(x + 1) + te, te)
+            copies.append(send(remote((name, "3l", m), piece, piece, left_mate)))
         yield
         on_right.wait_recv()
         on_left.wait_recv()
-        piece = block(tq * of4(x + 2), tq)
-        copies.append(send(remote((name, "c2", m), piece, piece, mate)))
-        yield copies
+        if not direct:
+            piece = block(tq * of4(x + 2), tq)
+            copies.append(send(remote((name, "c2", m), piece, piece, mate)))
+            yield
+        return copies
 
     def spread(m):
-        for copies in ring_gather("o", m, lambda start, size: out.at[out_block(m, start, size)]):
-            yield
+        copies = yield from ring_gather("o", m, lambda start, size: out.at[out_block(m, start, size)], DIRECT_OUT)
         for copy in copies:
             copy.wait_recv()
 
@@ -340,15 +355,27 @@
         copy.wait_recv()
         first = x_first(m, 1)
         yield
-        second = x_second(m, 1, first)
-        yield
-        x_last(m, 1, second)
-        pack(zs.at[m, 0], xsum[m, 0])
-        copy = send(remote(("z", 0, m), zs.at[m, 0], zr.at[m, 0], zmate))
-        yield
-        copy.wait_recv()
         rows = cols(tq * x, tq)
-        total = unpack(zs.at[m, 0], tq, half) + unpack(zr.at[m, 0], tq, half)
+        if m in FAST:
+            copies = x_second(m, 1, first, (right_z, left_z))
+            pack(zs.at[m, 0], x_block(m, 1, 0))
+            copies.append(send(remote(("z", 0, m), zs.at[m, 0], zr.at[m, 0], zmate)))
+            yield
+            for copy in copies:
+                copy.wait_recv()
+            used = pl.ds(0, tq * half // 128 + 16)
+            here = [unpack(part, tq, half) for part in (zs.at[m, 0], xr2.at[m, 0, used], xr2.at[m, 1, used])]
+            there = [unpack(part, tq, half) for part in (zr.at[m, 0], xr3.at[m, 0], xr3.at[m, 1])]
+            total = (here[0] + here[1] + here[2]) + (there[0] + there[1] + there[2])
+        else:
+            second = x_second(m, 1, first)
+            yield
+            x_last(m, 1, second)
+            pack(zs.at[m, 0], xsum[m, 0])
+            copy = send(remote(("z", 0, m), zs.at[m, 0], zr.at[m, 0], zmate))
+            yield
+            copy.wait_recv()
+            total = unpack(zs.at[m, 0], tq, half) + unpack(zr.at[m, 0], tq, half)
         grad_rows = pl.ds(pl.multiple_of(tok * (m % SPLIT) + tq * x, tq), tq)
         gs[m] = (total + gbuf[m // SPLIT, grad_rows, cols(half * core, half)]).astype(BF16)
         for copy in beyond_copies(m):
@@ -356,6 +383,8 @@
         pack(ds.at[m], total)
         send(cross_copy(m))
         out[out_block(m, tq * x, tq)] = total.astype(BF16)
+        for _ in range(HOLD * (chunks - 1 - m)):
+            yield
         yield from spread(m)
 
     def cross_copy(m):
@@ -394,8 +423,7 @@
     def up_chain(m):
         for copy in beyond_copies(m):
             copy.wait_recv()
-        for copies in ring_gather("g", m, lambda start, size: glow.at[m, :, core, cols(start, size)]):
-            yield
+        copies = yield from ring_gather("g", m, lambda start, size: glow.at[m, :, core, cols(start, size)], DIRECT)
         for copy in copies:
             copy.wait_recv()
         swaps = []
@@ -503,6 +531,7 @@
         vmem((chunks, 2, tq * tile // 128 + 16, 128), BF16),
         vmem((chunks, 2, tq * half // 128 + 16, 128), BF16),
         vmem((chunks, 2, tq * tile // 128 + 16, 128), BF16),
+        vmem((chunks, 2, tq * half // 128 + 16, 128), BF16),
         vmem((chunks, 2, tq, half), F32),
         vmem((chunks, 2, tq * half // 128 + 16, 128), BF16),
         vmem((chunks, 3, tq * half // 128 + 16, 128), BF16),

time: 115 us -> 111 us (0.965)
  Pallas kernels: 113 us -> 109 us
    pallas_call x1, Pallas kernels: 113 us -> 109 us  [local(): pl.pallas_call(kernel, out_shape=vmem((1, batches, whole, tile), BF16), i...]
where the time goes in v6:
time: 111 us
  Pallas kernels  109 us (98%)
  other arithmetic  2.12 us (2%)
    pallas_call x1, Pallas kernels, local(): pl.pallas_call(kernel, out_shape=vmem((1, batches, whole, tile), BF16), i...  109 us

profile of v6, /device:TPU:65, one launch (start us, length us, event | category | flops | bytes accessed | tf_op | source)
XLA Modules:
  0.0 111.3 jit_solution(10469290833751920692)
XLA Ops:
  0.0 0.0 copy-start
  0.0 109.2 %shard_map.46 = bf16[1,2,256,1536]{3,2,1,0:T(8,128)(2,1)S(1)} custom-call(f32[2,256,1536]{2,1,0:T(8,128)} %grad.1, bf16[1,1536,1536]{2,1,0:T(8,128)(2,1)} %win.1, bf16[1,1536,1536]{2,1,0:T(8,128)(2,1)} %wout.1, f32[1,2,256,1536]{3,2,1,0:T(8,128)} %pre.1), custom_call_target="tpu_custom_call" | custom-call | tf_op jit(solution)/shard_map/pallas_call | solution.py:545
  109.2 0.0 copy-done
  109.2 2.1 %bitcast_add_fusion = f32[1,2,256,1536]{3,2,1,0:T(8,128)} fusion(f32[2,256,1536]{2,1,0:T(8,128)S(1)} %copy-done, bf16[1,2,256,1536]{3,2,1,0:T(8,128)(2,1)S(1)} %shard_map.46), kind=kLoop, calls=%fused_computation | loop fusion | flops 1572864 | bytes 7864320 | tf_op jit(solution)/shard_map/add | solution.py:555
Async XLA Ops:
  0.0 109.2 %copy-start = (f32[2,256,1536]{2,1,0:T(8,128)S(1)}, f32[2,256,1536]{2,1,0:T(8,128)}, u32[]{:S(2)}) copy-start(f32[2,256,1536]{2,1,0:T(8,128)} %grad.1) | copy-start | bytes 9437188

commit v7 on v6

--- a/solution.py
+++ b/solution.py
@@ -14,12 +14,12 @@
 N_LOCAL = 32
 PIECES = 6
 DIRECT = True
-DIRECT_OUT = True
+DIRECT_OUT = False
 HOLD = 1
 FAST = (0,)
 SPLIT = 2
 START_DOWN = (0, 1, 2, 3)
-START_UP = (0, 1, 2, 2)
+START_UP = (0, 1, 2, 3)
 NT = (((1,), (1,)), ((), ()))
 
 

time: 111 us -> 115 us (1.036); the launches traced: 111 us -> 114 us
  Pallas kernels: 109 us -> 112 us
    pallas_call x1, Pallas kernels: 109 us -> 112 us  [local(): pl.pallas_call(kernel, out_shape=vmem((1, batches, whole, tile), BF16), i...]
where the time goes in v7:
time: 115 us; the launch traced here: 114 us
  Pallas kernels  112 us (97%)
  other arithmetic  2.12 us (2%)
    pallas_call x1, Pallas kernels, local(): pl.pallas_call(kernel, out_shape=vmem((1, batches, whole, tile), BF16), i...  112 us

profile of v7, /device:TPU:65, one launch (start us, length us, event | category | flops | bytes accessed | tf_op | source)
XLA Modules:
  0.0 113.9 jit_solution(11800151490793464414)
XLA Ops:
  0.0 0.0 copy-start
  0.0 111.8 %shard_map.46 = bf16[1,2,256,1536]{3,2,1,0:T(8,128)(2,1)S(1)} custom-call(f32[2,256,1536]{2,1,0:T(8,128)} %grad.1, bf16[1,1536,1536]{2,1,0:T(8,128)(2,1)} %win.1, bf16[1,1536,1536]{2,1,0:T(8,128)(2,1)} %wout.1, f32[1,2,256,1536]{3,2,1,0:T(8,128)} %pre.1), custom_call_target="tpu_custom_call" | custom-call | tf_op jit(solution)/shard_map/pallas_call | solution.py:545
  111.8 0.0 copy-done
  111.8 2.1 %bitcast_add_fusion = f32[1,2,256,1536]{3,2,1,0:T(8,128)} fusion(f32[2,256,1536]{2,1,0:T(8,128)S(1)} %copy-done, bf16[1,2,256,1536]{3,2,1,0:T(8,128)(2,1)S(1)} %shard_map.46), kind=kLoop, calls=%fused_computation | loop fusion | flops 1572864 | bytes 7864320 | tf_op jit(solution)/shard_map/add | solution.py:555
Async XLA Ops:
  0.0 111.8 %copy-start = (f32[2,256,1536]{2,1,0:T(8,128)S(1)}, f32[2,256,1536]{2,1,0:T(8,128)}, u32[]{:S(2)}) copy-start(f32[2,256,1536]{2,1,0:T(8,128)} %grad.1) | copy-start | bytes 9437188
